TPU v7x, 32 devices: a whole 2x2x4 slice. The times are simulated.
32 devices in a mesh: head: 4 (over y, x), space: 8 (over z, core).
Axes of the slice: x: 2, y: 2, z: 4, core: 2. Of those that a mesh axis runs over, the one named last changes fastest.
Arguments:
- features: bfloat16 [1024, 512, 256], P('space', 'head'), may hold values from -6 to 6
- stain_delta: float32 [256], replicated, may hold values from -0.4 to 0.4
- tissue: int32 [16, 8], P('space', 'head'), may hold values from 0 to 1, as said below
- reduce_weight: bfloat16 [256, 128], replicated, may hold values from -0.375 to 0.375
- spatial_weight: bfloat16 [3, 3, 128, 128], replicated, may hold values from -0.1875 to 0.1875
- expand_weight: bfloat16 [128, 512], replicated, may hold values from -0.5 to 0.5
- shortcut_weight: bfloat16 [256, 512], replicated, may hold values from -0.375 to 0.375
- attn_tanh: float32 [512, 256], replicated, may hold values from -1 to 1
- attn_sigm: float32 [512, 256], replicated, may hold values from -1 to 1
- attn_out: float32 [256], replicated, may hold values from -2 to 2
- classifier: float32 [512], replicated, may hold values from -0.75 to 0.75
- step_dir: int32 [256], replicated, may hold values from 0 to 1
Outputs:
- feature_grad: bfloat16 [1024, 512, 256], P('space', 'head')
- new_delta: float32 [256], replicated
Inputs may be any that keep to these rules, and one draw needn't show every extreme that they name: The tile at the slide's first row and column holds tissue.
All inputs are finite; a program needn't handle non-finite values.
Results may differ from a plain program's by a relative error of at most 0.0065.
Values may be sent and summed in bfloat16 or wider, within the bound.
A program may use at most 128 MiB of HBM per device.

v0:
```python
import functools

import jax
import jax.numpy as jnp
from jax import lax
from jax.experimental import pallas as pl
from jax.experimental.pallas import tpu as pltpu
from jax.sharding import PartitionSpec as P

TILE = 64
ALPHA = 1
BLOCK = 16
SUB = 8
F32 = jnp.float32
BF16 = jnp.bfloat16
HP = lax.Precision.HIGHEST


def sigm(value):
    return 0.5 + 0.5 * jnp.tanh(0.5 * value)


def passed_along(value, axis, steps):
    count = lax.axis_size(axis)
    first, last = (max(0, -steps), min(count, count - steps))
    return lax.ppermute(value, axis, [(source, source + steps) for source in range(first, last)])


def dot(a, b):
    return jnp.dot(a, b, preferred_element_type=F32)


def forward_kernel(
    tiles_r, tiles_c, x_ref, up_ref, left_ref, wr_ref, wc_ref, wp_ref, at_ref, as_ref, ao_ref, live_ref,
    slope1_ref, slope2_ref, slope3_ref, pay_ref, embed_ref, tval_ref, gval_ref, score_ref,
    red, lo, hi, taps, sums,
):
    step = pl.program_id(0)
    rows, cols, chan = x_ref.shape
    mid = wr_ref.shape[1]
    cout = wp_ref.shape[1]
    orow, ocol = rows // 2, cols // 2
    half = TILE // 2

    def put_taps(slot, source):
        for b, start in enumerate((SUB - 1, SUB, SUB + 1)):
            taps[slot, :, b * mid : (b + 1) * mid] = source[pl.ds(start, ocol, stride=2), :].astype(BF16)

    @pl.when(step == 0)
    def _():
        put_taps(0, up_ref)
        sums[...] = jnp.zeros_like(sums)

    @pl.when(step > 0)
    def _():
        taps[0] = taps[rows]

    pre = dot(x_ref[...].reshape(rows * cols, chan), wr_ref[...])
    sig = sigm(pre)
    act = pre * sig
    slope1_ref[...] = (sig + act * (1.0 - sig)).reshape(rows, cols, mid).astype(BF16)
    red[:, SUB:, :] = act.reshape(rows, cols, mid)
    red[:, SUB - 1 : SUB, :] = left_ref[...]
    for r in range(rows):
        put_taps(r + 1, red.at[r])
    acc = jnp.zeros((orow * ocol, mid), F32)
    for a in range(3):
        part = jnp.stack([taps[2 * i + a] for i in range(orow)], axis=0)
        acc = acc + dot(part.reshape(orow * ocol, 3 * mid), wc_ref[a])
    sig = sigm(acc)
    act = acc * sig
    slope2_ref[...] = (sig + act * (1.0 - sig)).reshape(orow, ocol, mid).astype(BF16)
    short = []
    for i in range(orow):
        lo[i] = x_ref[2 * i, :, : chan // 2].astype(F32)
        hi[i] = x_ref[2 * i, :, chan // 2 :].astype(F32)
    for i in range(orow):
        short.append(
            jnp.concatenate(
                [lo.at[i][pl.ds(0, ocol, stride=2), :].astype(BF16), hi.at[i][pl.ds(0, ocol, stride=2), :].astype(BF16)],
                axis=1,
            )
        )
    short = jnp.stack(short, axis=0).reshape(orow * ocol, chan)
    preact = dot(jnp.concatenate([act.astype(BF16), short], axis=1), wp_ref[...])
    sig = sigm(preact)
    act = preact * sig
    slope3_ref[...] = (sig + act * (1.0 - sig)).reshape(orow, ocol, cout).astype(BF16)
    cells = jnp.sum(act.reshape(orow, tiles_c, half // SUB, SUB, cout), axis=(0, 2))
    trow = (step * orow) // half
    for c in range(tiles_c):
        slot = trow * tiles_c + c
        sums[slot] = sums[slot] + cells[c]

    @pl.when(step == pl.num_programs(0) - 1)
    def _():
        embed = jnp.sum(sums[...], axis=1) * (1.0 / (half * half))
        tval = jnp.tanh(jnp.dot(embed, at_ref[...], precision=HP, preferred_element_type=F32))
        gval = sigm(jnp.dot(embed, as_ref[...], precision=HP, preferred_element_type=F32))
        score = jnp.sum(tval * gval * ao_ref[...], axis=1, keepdims=True)
        live = live_ref[:, 0:1] > 0
        top = jnp.max(jnp.where(live, score, -1e30), axis=0, keepdims=True)
        weight = jnp.where(live, jnp.exp(score - top), 0.0)
        pay_ref[0:1, :] = jnp.sum(weight * embed, axis=0, keepdims=True)
        pay_ref[1:2, :] = jnp.broadcast_to(jnp.sum(weight, axis=0, keepdims=True), (1, cout))
        pay_ref[2:3, :] = jnp.broadcast_to(top, (1, cout))
        pay_ref[3:8, :] = jnp.zeros((5, cout), F32)
        embed_ref[...] = embed
        tval_ref[...] = tval
        gval_ref[...] = gval
        score_ref[...] = jnp.broadcast_to(score, score_ref.shape)


def exchange_kernel(sizes, softmax, pay_ref, out_ref, got0, got1, mine, send0, send1, recv0, recv1):
    axes = ("head", "space")
    place = tuple(lax.axis_index(axis) for axis in axes)
    gots, sends, recvs = (got0, got1), (send0, send1), (recv0, recv1)

    def peer(k, hop):
        other = lax.rem(place[k] + hop, sizes[k])
        return (other, place[1]) if k == 0 else (place[0], other)

    barrier = pltpu.get_barrier_semaphore()
    for k in range(2):
        @pl.loop(1, sizes[k])
        def _(hop):
            pl.semaphore_signal(barrier, inc=1, device_id=peer(k, hop), device_id_type=pl.DeviceIdType.MESH)
    pl.semaphore_wait(barrier, sizes[0] + sizes[1] - 2)

    mine[0] = pay_ref[...]
    for k in range(2):
        got, n = gots[k], sizes[k]

        def copy(hop):
            return pltpu.make_async_remote_copy(
                src_ref=mine.at[k],
                dst_ref=got.at[hop],
                send_sem=sends[k].at[hop],
                recv_sem=recvs[k].at[hop],
                device_id=peer(k, hop),
                device_id_type=pl.DeviceIdType.MESH,
            )

        @pl.loop(1, n)
        def _(hop):
            copy(hop).start()

        got[0] = mine[k]

        @pl.loop(1, n)
        def _(hop):
            copy(hop).wait()

        every = got[...]
        if softmax:
            top = jnp.max(every[:, 2:3, :], axis=0)
            factor = jnp.exp(every[:, 2:3, :] - top[None])
            total = jnp.sum(every[:, 0:2, :] * factor, axis=0)
            result = jnp.concatenate([total, top, jnp.zeros((5, top.shape[1]), F32)], axis=0)
        else:
            result = jnp.sum(every, axis=0)
        if k == 0:
            mine[1] = result
        else:
            out_ref[...] = result


def exchange(payload, softmax, ident):
    sizes = (lax.axis_size("head"), lax.axis_size("space"))
    return pl.pallas_call(
        functools.partial(exchange_kernel, sizes, softmax),
        out_shape=jax.ShapeDtypeStruct(payload.shape, F32),
        in_specs=[pl.BlockSpec(memory_space=pltpu.VMEM)],
        out_specs=pl.BlockSpec(memory_space=pltpu.VMEM),
        scratch_shapes=[
            pltpu.VMEM((sizes[0],) + payload.shape, F32),
            pltpu.VMEM((sizes[1],) + payload.shape, F32),
            pltpu.VMEM((2,) + payload.shape, F32),
            pltpu.SemaphoreType.DMA((sizes[0],)),
            pltpu.SemaphoreType.DMA((sizes[1],)),
            pltpu.SemaphoreType.DMA((sizes[0],)),
            pltpu.SemaphoreType.DMA((sizes[1],)),
        ],
        compiler_params=pltpu.CompilerParams(collective_id=ident, has_side_effects=True),
        name="exchange_softmax" if softmax else "exchange_sum",
    )(payload)


def spread(dembed_ref, first, tiles_c, half):
    cout = dembed_ref.shape[1]
    return jnp.concatenate(
        [jnp.broadcast_to(dembed_ref[pl.ds(first + c, 1), :], (half, cout)) for c in range(tiles_c)], axis=0
    )


def edge_kernel(
    tiles_r, tiles_c, comb_ref, embed_ref, tval_ref, gval_ref, score_ref, live_ref, ao_ref, cls_ref, at_ref, as_ref,
    we_ref, row3_ref, row2_ref, col3_ref, col2_ref, dembed_ref, drow_ref, dcol_ref,
):
    half = TILE // 2
    embed, tval, gval = embed_ref[...], tval_ref[...], gval_ref[...]
    ao, cls = ao_ref[...], cls_ref[...]
    pooled = comb_ref[0:1, :] / comb_ref[1:2, :]
    total, top = comb_ref[1:2, 0:1], comb_ref[2:3, 0:1]
    live = live_ref[:, 0:1] > 0
    prob = jnp.where(live, jnp.exp(score_ref[:, 0:1] - top), 0.0) / total
    gap = jnp.sum(embed * cls, axis=1, keepdims=True) - jnp.sum(pooled * cls, axis=1, keepdims=True)
    datt = (prob * gap) * ao
    dtanh = datt * gval * (1.0 - tval * tval)
    dsigm = datt * tval * gval * (1.0 - gval)
    back = (((1,), (1,)), ((), ()))
    dembed = (
        prob * cls
        + lax.dot_general(dtanh, at_ref[...], back, precision=HP, preferred_element_type=F32)
        + lax.dot_general(dsigm, as_ref[...], back, precision=HP, preferred_element_type=F32)
    )
    dembed_ref[...] = dembed * (1.0 / (half * half))
    dpre = (row3_ref[0].astype(F32) * spread(dembed_ref, 0, tiles_c, half)).astype(BF16)
    drow_ref[...] = (dot(dpre, we_ref[...]) * row2_ref[0].astype(F32)).astype(BF16)
    cout = embed.shape[1]
    down = jnp.concatenate(
        [jnp.broadcast_to(dembed_ref[r * tiles_c : r * tiles_c + 1, :], (half, cout)) for r in range(tiles_r)], axis=0
    )
    dpre = (col3_ref[...].astype(F32) * down).astype(BF16)
    dcol_ref[...] = (dot(dpre, we_ref[...]) * col2_ref[...].astype(F32)).astype(BF16)


def backward_kernel(
    tiles_c, x_ref, slope1_ref, slope2_ref, slope3_ref, dembed_ref, right_ref, low_ref, wb_ref, wt_ref, wo_ref,
    out_ref, grad_ref, dsx, drs, slo, shi,
):
    step = pl.program_id(0)
    rows, cols, chan = x_ref.shape
    orow, ocol, mid = slope2_ref.shape
    cout = slope3_ref.shape[2]
    half = TILE // 2
    block = pl.num_programs(0) - 1 - step
    trow = (block * orow) // half

    @pl.when(step == 0)
    def _():
        dsx[orow] = low_ref[...]
        slo[...] = jnp.zeros_like(slo)
        shi[...] = jnp.zeros_like(shi)
        grad_ref[...] = jnp.zeros_like(grad_ref)

    @pl.when(step > 0)
    def _():
        dsx[orow] = dsx[0]

    dpre = (slope3_ref[...].astype(F32) * spread(dembed_ref, trow * tiles_c, tiles_c, half)[None]).astype(BF16)
    both = dot(dpre.reshape(orow * ocol, cout), wb_ref[...])
    dsx[0:orow, 0:ocol, :] = both[:, :mid].reshape(orow, ocol, mid) * slope2_ref[...].astype(F32)
    dsx[0:orow, ocol : ocol + 1, :] = right_ref[...]
    for i in range(orow):
        slo[i, pl.ds(0, ocol, stride=2), :] = both[i * ocol : (i + 1) * ocol, mid : mid + chan // 2]
        shi[i, pl.ds(0, ocol, stride=2), :] = both[i * ocol : (i + 1) * ocol, mid + chan // 2 :]
    four = jnp.concatenate(
        [
            dsx[di : di + orow, dj : dj + ocol, :].astype(BF16).reshape(orow * ocol, mid)
            for di in range(2)
            for dj in range(2)
        ],
        axis=1,
    )
    grads = dot(four, wt_ref[...])
    for i in range(orow):
        for di in range(2):
            for dj in range(2):
                n = 2 * di + dj
                drs[2 * i + di, pl.ds(dj, ocol, stride=2), :] = grads[i * ocol : (i + 1) * ocol, n * mid : (n + 1) * mid]
    dred = (drs[...] * slope1_ref[...].astype(F32)).astype(BF16)
    dinput = dot(dred.reshape(rows * cols, mid), wo_ref[...]).reshape(rows, cols, chan)
    total = jnp.zeros((SUB, chan), F32)
    for r in range(rows):
        value = dinput[r]
        if r % 2 == 0:
            value = value + jnp.concatenate([slo[r // 2], shi[r // 2]], axis=1)
        out_ref[r] = value.astype(BF16)
        total = total + jnp.sum((value * x_ref[r].astype(F32)).reshape(cols // SUB, SUB, chan), axis=0)
    grad_ref[...] += total


def whole(shape):
    return pl.BlockSpec(shape, lambda i: (0,) * len(shape))


def shards(
    features,
    stain_delta,
    tissue,
    reduce_weight,
    spatial_weight,
    expand_weight,
    shortcut_weight,
    attn_tanh,
    attn_sigm,
    attn_out,
    classifier,
    step_dir,
):
    rows, cols, chan = features.shape
    mid = reduce_weight.shape[1]
    cout = expand_weight.shape[1]
    att = attn_out.shape[0]
    tiles_r, tiles_c = tissue.shape
    slots = -(-tiles_r * tiles_c // SUB) * SUB
    orow, ocol = rows // 2, cols // 2
    scale = 1.0 + stain_delta
    wide = scale[:, None]
    wr = (reduce_weight.astype(F32) * wide).astype(BF16)
    ws = (shortcut_weight.astype(F32) * wide).astype(BF16)
    wc = spatial_weight.reshape(3, 3 * mid, mid)
    wp = jnp.concatenate([expand_weight, ws], axis=0)
    wb = jnp.concatenate([expand_weight.T, ws.T], axis=1)
    wo = wr.T
    none = jnp.zeros((mid, mid), BF16)

    def turned(a, b):
        return spatial_weight[a, b].T

    wt = jnp.concatenate(
        [
            jnp.concatenate([turned(1, 1), turned(1, 2), turned(2, 1), turned(2, 2)], axis=1),
            jnp.concatenate([none, turned(1, 0), none, turned(2, 0)], axis=1),
            jnp.concatenate([none, none, turned(0, 1), turned(0, 2)], axis=1),
            jnp.concatenate([none, none, none, turned(0, 0)], axis=1),
        ],
        axis=0,
    )
    live = jnp.pad((tissue.reshape(-1, 1) > 0).astype(F32), ((0, slots - tiles_r * tiles_c), (0, 127)))
    ao = attn_out[None, :]
    cls = classifier[None, :]

    rim = dot(jnp.concatenate([features[-1], features[:, -1]], axis=0), wr)
    rim = jax.nn.silu(rim).astype(BF16)
    upper = passed_along(rim[:cols], "space", 1)
    left = passed_along(jnp.concatenate([upper[-1:], rim[cols:]], axis=0), "head", 1).astype(F32)
    up = jnp.concatenate([jnp.zeros((SUB - 1, mid), F32), left[:1], upper.astype(F32)], axis=0)
    left = left[1:, None]

    steps = rows // BLOCK
    params = pltpu.CompilerParams(dimension_semantics=("arbitrary",), vmem_limit_bytes=56 * 1024 * 1024)
    slope1, slope2, slope3, pay, embed, tval, gval, score = pl.pallas_call(
        functools.partial(forward_kernel, tiles_r, tiles_c),
        grid=(steps,),
        out_shape=(
            jax.ShapeDtypeStruct((rows, cols, mid), BF16),
            jax.ShapeDtypeStruct((orow, ocol, mid), BF16),
            jax.ShapeDtypeStruct((orow, ocol, cout), BF16),
            jax.ShapeDtypeStruct((SUB, cout), F32),
            jax.ShapeDtypeStruct((slots, cout), F32),
            jax.ShapeDtypeStruct((slots, att), F32),
            jax.ShapeDtypeStruct((slots, att), F32),
            jax.ShapeDtypeStruct((slots, 128), F32),
        ),
        in_specs=[
            pl.BlockSpec((BLOCK, cols, chan), lambda i: (i, 0, 0)),
            whole(up.shape),
            pl.BlockSpec((BLOCK, 1, mid), lambda i: (i, 0, 0)),
            whole(wr.shape),
            whole(wc.shape),
            whole(wp.shape),
            whole(attn_tanh.shape),
            whole(attn_sigm.shape),
            whole(ao.shape),
            whole(live.shape),
        ],
        out_specs=(
            pl.BlockSpec((BLOCK, cols, mid), lambda i: (i, 0, 0)),
            pl.BlockSpec((BLOCK // 2, ocol, mid), lambda i: (i, 0, 0)),
            pl.BlockSpec((BLOCK // 2, ocol, cout), lambda i: (i, 0, 0)),
            whole((SUB, cout)),
            whole((slots, cout)),
            whole((slots, att)),
            whole((slots, att)),
            whole((slots, 128)),
        ),
        scratch_shapes=[
            pltpu.VMEM((BLOCK, cols + SUB, mid), F32),
            pltpu.VMEM((BLOCK // 2, cols, chan // 2), F32),
            pltpu.VMEM((BLOCK // 2, cols, chan // 2), F32),
            pltpu.VMEM((BLOCK + 1, ocol, 3 * mid), BF16),
            pltpu.VMEM((slots, SUB, cout), F32),
        ],
        compiler_params=params,
        name="forward",
    )(features, up, left, wr, wc, wp, attn_tanh, attn_sigm, ao, live)

    comb = exchange(pay, True, 0)

    we = wb[:, :mid]
    row3, row2, col3, col2 = slope3[:1], slope2[:1], slope3[:, 0], slope2[:, 0]
    dembed, drow, dcol = pl.pallas_call(
        functools.partial(edge_kernel, tiles_r, tiles_c),
        out_shape=(
            jax.ShapeDtypeStruct((slots, cout), F32),
            jax.ShapeDtypeStruct((ocol, mid), BF16),
            jax.ShapeDtypeStruct((orow, mid), BF16),
        ),
        name="edge",
    )(comb, embed, tval, gval, score, live, ao, cls, attn_tanh, attn_sigm, we, row3, row2, col3, col2)
    below = passed_along(drow, "space", -1)
    right = passed_along(jnp.concatenate([dcol, below[:1]], axis=0), "head", -1).astype(F32)
    low = jnp.concatenate([below.astype(F32), right[-1:], jnp.zeros((SUB - 1, mid), F32)], axis=0)
    right = right[:-1, None]

    def turn(i):
        return (steps - 1 - i, 0, 0)

    feature_grad, partial_grad = pl.pallas_call(
        functools.partial(backward_kernel, tiles_c),
        grid=(steps,),
        out_shape=(
            jax.ShapeDtypeStruct((rows, cols, chan), BF16),
            jax.ShapeDtypeStruct((SUB, chan), F32),
        ),
        in_specs=[
            pl.BlockSpec((BLOCK, cols, chan), turn),
            pl.BlockSpec((BLOCK, cols, mid), turn),
            pl.BlockSpec((BLOCK // 2, ocol, mid), turn),
            pl.BlockSpec((BLOCK // 2, ocol, cout), turn),
            whole(dembed.shape),
            pl.BlockSpec((BLOCK // 2, 1, mid), turn),
            whole(low.shape),
            whole(wb.shape),
            whole(wt.shape),
            whole(wo.shape),
        ],
        out_specs=(pl.BlockSpec((BLOCK, cols, chan), turn), whole((SUB, chan))),
        scratch_shapes=[
            pltpu.VMEM((BLOCK // 2 + 1, ocol + SUB, mid), F32),
            pltpu.VMEM((BLOCK, cols, mid), F32),
            pltpu.VMEM((BLOCK // 2, cols, chan // 2), F32),
            pltpu.VMEM((BLOCK // 2, cols, chan // 2), F32),
        ],
        compiler_params=params,
        name="backward",
    )(features, slope1, slope2, slope3, dembed, right, low, wb, wt, wo)

    ddelta = jnp.sum(exchange(partial_grad, False, 1), axis=0) / scale
    norm_size = jnp.sqrt(jnp.mean(ddelta * ddelta) + 1e-06)
    direction = (2 * step_dir - 1).astype(F32)
    new_delta = stain_delta + direction * float(ALPHA) * ddelta / norm_size
    return (feature_grad, new_delta)


def solution(mesh):
    return jax.shard_map(
        shards,
        mesh=mesh,
        in_specs=(P("space", "head", None), P(), P("space", "head")) + (P(),) * 9,
        out_specs=(P("space", "head", None), P()),
        check_vma=False,
    )
```

profile of v0, /device:TPU:0, one launch (start us, length us, event | category | flops | bytes accessed | tf_op | source)
XLA Modules:
  0.0 109.3 jit_solution(16227923867043065582)
XLA Ops:
  0.6 0.8 slice_bitcast_fusion.1
  1.5 1.2 %slice.70 = bf16[128,1,256]{2,1,0:T(2,128)(2,1)S(1)} slice(bf16[128,128,256]{2,1,0:T(8,128)(2,1)} %x_ref.3), slice={[0:128], [127:128], [0:256]} | slice | bytes 131072 | tf_op jit(solution)/shard_map/slice | solution.py:335
  2.7 0.7 broadcast_add_fusion
  3.3 0.9 copy.34
  4.6 2.4 %collective-permute-start = (bf16[128,128]{1,0:T(8,128)(2,1)S(1)}, bf16[128,128]{1,0:T(8,128)(2,1)S(1)}, u32[]{:S(2)}, u32[]{:S(2)}) collective-permute-start(bf16[128,128]{1,0:T(8,128)(2,1)S(1)} %get-tuple-element.38), channel_id=1, source_target_pairs={{0,1},{1,2},{2,3},{3,4},{4,5},{5,6},{6,7},{8,9},{9,10},{10,11},{11... | collective-permute-start | bytes 98312 | tf_op jit(solution)/shard_map/ppermute | solution.py:26
  6.9 0.6 fusion.13.wo_ref
  7.6 1.1 copy.35
  8.8 0.7 broadcast_compare_fusion
  9.4 1.0 copy.36
  10.5 1.0 fusion.10
  11.6 4.2 %collective-permute-start.1 = (bf16[129,128]{1,0:T(8,128)(2,1)S(1)}, bf16[129,128]{1,0:T(8,128)(2,1)S(1)}, u32[]{:S(2)}, u32[]{:S(2)}) collective-permute-start(bf16[129,128]{1,0:T(8,128)(2,1)S(1)} %pad_maximum_fusion.4), channel_id=1, source_target_pairs={{0,8},{8,16},{16,24},{1,9},{9,17},{17,25},{2,10},{10,18},{18,26},{... | collective-permute-start | bytes 99080 | tf_op jit(solution)/shard_map/ppermute | solution.py:26
  16.5 0.7 copy.38.wr_ref
  17.2 0.9 copy.39.wp_ref
  19.3 0.6 pad_maximum_fusion.2.up_ref
  20.5 19.5 %forward.1 = (bf16[128,128,128]{2,1,0:T(8,128)(2,1)}, bf16[64,64,128]{2,1,0:T(8,128)(2,1)}, bf16[64,64,512]{2,1,0:T(8,128)(2,1)}, f32[8,512]{1,0:T(8,128)}, f32[...) custom-call(bf16[128,128,256]{2,1,0:T(8,128)(2,1)} %x_ref.3, ...), custom_call_target="tpu_custom_call" | custom-call | tf_op jit(solution)/shard_map/forward/pallas_call | solution.py:344
  40.1 1.3 %slice.77.row2_ref = bf16[1,64,128]{2,1,0:T(8,128)(2,1)} slice(bf16[64,64,128]{2,1,0:T(8,128)(2,1)} %get-tuple-element.16.slope2_ref), slice={[0:1], [0:64], [0:128]} | slice | bytes 32768 | tf_op jit(solution)/shard_map/slice | solution.py:393
  41.4 1.9 %copy.42 = bf16[64,64,128]{2,0,1:T(8,128)(2,1)S(1)} copy(bf16[64,64,128]{2,1,0:T(8,128)(2,1)} %get-tuple-element.16.slope2_ref) | data formatting | bytes 2097152 | tf_op jit(solution)/shard_map/forward/pallas_call | solution.py:344
  43.3 1.5 %slice.76.row3_ref = bf16[1,64,512]{2,1,0:T(8,128)(2,1)} slice(bf16[64,64,512]{2,1,0:T(8,128)(2,1)} %get-tuple-element.17.slope3_ref), slice={[0:1], [0:64], [0:512]} | slice | bytes 131072 | tf_op jit(solution)/shard_map/slice | solution.py:393
  44.8 6.6 %copy.41 = bf16[64,64,512]{2,0,1:T(8,128)(2,1)} copy(bf16[64,64,512]{2,1,0:T(8,128)(2,1)} %get-tuple-element.17.slope3_ref) | data formatting | bytes 8388608 | tf_op jit(solution)/shard_map/forward/pallas_call | solution.py:344
  51.4 12.0 %exchange_softmax.1.comb_ref = f32[8,512]{1,0:T(8,128)} custom-call(f32[8,512]{1,0:T(8,128)} %get-tuple-element.18.pay_ref), custom_call_target="tpu_custom_call" | custom-call | tf_op jit(solution)/shard_map/exchange_softmax/pallas_call | solution.py:170
  64.0 1.5 %slice_bitcast_fusion.col3_ref = bf16[64,512]{1,0:T(8,128)(2,1)} fusion(bf16[64,64,512]{2,0,1:T(8,128)(2,1)} %copy.41), kind=kLoop, calls=%fused_computation.13 | loop fusion | bytes 131072 | tf_op jit(solution)/shard_map/squeeze | solution.py:393
  65.5 3.1 %edge.1 = (f32[8,512]{1,0:T(8,128)}, bf16[64,128]{1,0:T(8,128)(2,1)}, bf16[64,128]{1,0:T(8,128)(2,1)}) custom-call(f32[8,512]{1,0:T(8,128)} %exchange_softmax.1.comb_ref, f32[8,512]{1,0:T(8,128)} %get-tuple-element.19.embed_ref, f32[8,256]{1,0:T(8,128)} %get-tuple-element.20.tval_ref, f32[8,256]{1,0:T(8,128)} %get-tuple-element.21.gval_ref, ...), custom_call_target="tpu_custom_call" | custom-call | tf_op jit(solution)/shard_map/edge/pallas_call | solution.py:394
  68.6 1.3 %collective-permute-start.2 = (bf16[64,128]{1,0:T(8,128)(2,1)}, bf16[64,128]{1,0:T(8,128)(2,1)S(1)}, u32[]{:S(2)}, u32[]{:S(2)}) collective-permute-start(bf16[64,128]{1,0:T(8,128)(2,1)} %get-tuple-element.25), channel_id=1, source_target_pairs={{1,0},{2,1},{3,2},{4,3},{5,4},{6,5},{7,6},{9,8},{10,9},{11,10},{12... | collective-permute-start | bytes 49160 | tf_op jit(solution)/shard_map/ppermute | solution.py:26
  69.9 0.8 fusion.1.wt_ref
  70.8 1.2 %collective-permute-done.2 = bf16[64,128]{1,0:T(8,128)(2,1)S(1)} collective-permute-done((bf16[64,128]{1,0:T(8,128)(2,1)}, bf16[64,128]{1,0:T(8,128)(2,1)S(1)}, u32[]{:S(2)}, u32[]{:S(2)}) %collective-permute-start.2) | collective-permute-done | bytes 16416 | tf_op jit(solution)/shard_map/ppermute | solution.py:26
  72.0 0.7 pad_maximum_fusion.5
  72.7 1.3 %collective-permute-start.3 = (bf16[65,128]{1,0:T(8,128)(2,1)S(1)}, bf16[65,128]{1,0:T(8,128)(2,1)S(1)}, u32[]{:S(2)}, u32[]{:S(2)}) collective-permute-start(bf16[65,128]{1,0:T(8,128)(2,1)S(1)} %pad_maximum_fusion.5), channel_id=1, source_target_pairs={{8,0},{16,8},{24,16},{9,1},{17,9},{25,17},{10,2},{18,10},{26,18},{... | collective-permute-start | bytes 49928 | tf_op jit(solution)/shard_map/ppermute | solution.py:26
  74.0 0.8 pad_maximum_fusion.1.wb_ref
  74.8 3.5 %collective-permute-done.3 = bf16[65,128]{1,0:T(8,128)(2,1)S(1)} collective-permute-done((bf16[65,128]{1,0:T(8,128)(2,1)S(1)}, bf16[65,128]{1,0:T(8,128)(2,1)S(1)}, u32[]{:S(2)}, u32[]{:S(2)}) %collective-permute-start.3) | collective-permute-done | bytes 16672 | tf_op jit(solution)/shard_map/ppermute | solution.py:26
  79.6 15.2 %backward.1 = (bf16[128,128,256]{2,1,0:T(8,128)(2,1)}, f32[8,256]{1,0:T(8,128)}) custom-call(bf16[128,128,256]{2,1,0:T(8,128)(2,1)} %x_ref.3, bf16[128,128,128]{2,1,0:T(8,128)(2,1)} %get-tuple-element.15.slope1_ref, bf16[64,64,128]{2,1,0:T(8,128)(2,1)} %get-tuple-element.16.slope2_ref, bf16[64,64,512]{2,1,0:T(8,128)(2,1)} %get-tuple-element.17.slope3_ref, ...), custom_call_target="tpu_custom_call" | custom-call | tf_op jit(solution)/shard_map/backward/pallas_call | solution.py:411
  94.8 11.9 %exchange_sum.1 = f32[8,256]{1,0:T(8,128)} custom-call(f32[8,256]{1,0:T(8,128)} %get-tuple-element.27.pay_ref), custom_call_target="tpu_custom_call" | custom-call | tf_op jit(solution)/shard_map/exchange_sum/pallas_call | solution.py:170
  106.7 0.7 reduce_sum.18
  (44 shorter events, 5.9 us)
Async XLA Ops:
  4.6 7.0 %collective-permute-start = (bf16[128,128]{1,0:T(8,128)(2,1)S(1)}, bf16[128,128]{1,0:T(8,128)(2,1)S(1)}, u32[]{:S(2)}, u32[]{:S(2)}) collective-permute-start(bf16[128,128]{1,0:T(8,128)(2,1)S(1)} %get-tuple-element.38), channel_id=1, source_target_pairs={{0,1},{1,2},{2,3},{3,4},{4,5},{5,6},{6,7},{8,9},{9,10},{10,11},{11... | collective-permute-start | bytes 98312 | tf_op jit(solution)/shard_map/ppermute | solution.py:26
  10.5 29.6 %copy-start = (bf16[128,512]{0,1:T(8,128)(2,1)}, bf16[128,512]{0,1:T(8,128)(2,1)S(1)}, u32[]{:S(2)}) copy-start(bf16[128,512]{0,1:T(8,128)(2,1)S(1)} %copy.36) | copy-start | bytes 393220
  11.6 7.6 %collective-permute-start.1 = (bf16[129,128]{1,0:T(8,128)(2,1)S(1)}, bf16[129,128]{1,0:T(8,128)(2,1)S(1)}, u32[]{:S(2)}, u32[]{:S(2)}) collective-permute-start(bf16[129,128]{1,0:T(8,128)(2,1)S(1)} %pad_maximum_fusion.4), channel_id=1, source_target_pairs={{0,8},{8,16},{16,24},{1,9},{9,17},{17,25},{2,10},{10,18},{18,26},{... | collective-permute-start | bytes 99080 | tf_op jit(solution)/shard_map/ppermute | solution.py:26
  44.8 29.2 %copy-start.1 = (bf16[128,512]{0,1:T(8,128)(2,1)S(1)}, bf16[128,512]{0,1:T(8,128)(2,1)}, u32[]{:S(2)}) copy-start(bf16[128,512]{0,1:T(8,128)(2,1)} %copy-done) | copy-start | bytes 393220
  68.6 3.4 %collective-permute-start.2 = (bf16[64,128]{1,0:T(8,128)(2,1)}, bf16[64,128]{1,0:T(8,128)(2,1)S(1)}, u32[]{:S(2)}, u32[]{:S(2)}) collective-permute-start(bf16[64,128]{1,0:T(8,128)(2,1)} %get-tuple-element.25), channel_id=1, source_target_pairs={{1,0},{2,1},{3,2},{4,3},{5,4},{6,5},{7,6},{9,8},{10,9},{11,10},{12... | collective-permute-start | bytes 49160 | tf_op jit(solution)/shard_map/ppermute | solution.py:26
  72.7 5.6 %collective-permute-start.3 = (bf16[65,128]{1,0:T(8,128)(2,1)S(1)}, bf16[65,128]{1,0:T(8,128)(2,1)S(1)}, u32[]{:S(2)}, u32[]{:S(2)}) collective-permute-start(bf16[65,128]{1,0:T(8,128)(2,1)S(1)} %pad_maximum_fusion.5), channel_id=1, source_target_pairs={{8,0},{16,8},{24,16},{9,1},{17,9},{25,17},{10,2},{18,10},{26,18},{... | collective-permute-start | bytes 49928 | tf_op jit(solution)/shard_map/ppermute | solution.py:26
  79.6 27.9 %copy-start.2 = (f32[256]{0:T(256)S(1)}, f32[256]{0:T(256)}, u32[]{:S(2)}) copy-start(f32[256]{0:T(256)} %param.13) | copy-start | bytes 3076
  79.6 29.2 %copy-start.3 = (s32[256]{0:T(256)S(1)}, s32[256]{0:T(256)}, u32[]{:S(2)}) copy-start(s32[256]{0:T(256)} %param.23) | copy-start | bytes 3076
where the time goes:
time: 110 us; the launch traced here: 109 us
  Pallas kernels  61.8 us (56%)
  local copies, waits for them, and re-layouts  23.5 us (21%)
  starting transfers between devices  9.14 us (8%)
  other arithmetic  8.31 us (8%)
  waiting for transfers between devices  4.76 us (4%)
  between operations  1.61 us (1%)
    pallas_call x2, Pallas kernels, exchange(): pl.pallas_call(functools.partial(exchange_kernel, sizes, softmax), out_sh...  23.9 us
    pallas_call x1, Pallas kernels, shards(): pl.pallas_call(functools.partial(forward_kernel, tiles_r, tiles_c), grid=...  19.5 us
    pallas_call x1, Pallas kernels, shards(): pl.pallas_call(functools.partial(backward_kernel, tiles_c), grid=(steps,)...  15.2 us
    ppermute x4, starting transfers between devices, passed_along(): lax.ppermute(value, axis, [(source, source + steps) for source in range(f...  9.14 us
    pallas_call x2, local copies, waits for them, and re-layouts, shards(): pl.pallas_call(functools.partial(forward_kernel, tiles_r, tiles_c), grid=...  8.48 us
    ppermute x4, waiting for transfers between devices, passed_along(): lax.ppermute(value, axis, [(source, source + steps) for source in range(f...  4.76 us
    unnamed x21, local copies, waits for them, and re-layouts  4.14 us
    pallas_call x1, Pallas kernels, shards(): pl.pallas_call(functools.partial(edge_kernel, tiles_r, tiles_c), out_shap...  3.15 us
  transfers between devices with their start and end apart: 4, of which 2 were waited for; matrix products, arithmetic and copies ran while one was open for 9% of the time, Pallas kernels for 0%

commit v1 on v0

v1 whole, which is shorter than its diff:
```python
import functools

import jax
import jax.numpy as jnp
from jax import lax
from jax.experimental import pallas as pl
from jax.experimental.pallas import tpu as pltpu
from jax.sharding import PartitionSpec as P

TILE = 64
ALPHA = 1
BLOCK = 16
SUB = 8
F32 = jnp.float32
MESH = pl.DeviceIdType.MESH
BF16 = jnp.bfloat16
HP = lax.Precision.HIGHEST


def sigm(value):
    return 0.5 + 0.5 * jnp.tanh(0.5 * value)


def passed_along(value, axis, steps):
    count = lax.axis_size(axis)
    first, last = (max(0, -steps), min(count, count - steps))
    return lax.ppermute(value, axis, [(source, source + steps) for source in range(first, last)])


def dot(a, b):
    return jnp.dot(a, b, preferred_element_type=F32)


def column(row, width):
    return jnp.transpose(jnp.broadcast_to(row, (width, row.shape[1])))


def rim_kernel(row_ref, col_ref, delta_ref, w_ref, row_out, col_out, corner_out):
    mid = w_ref.shape[1]
    wr = (w_ref[...].astype(F32) * column(1.0 + delta_ref[...], mid)).astype(BF16)
    row = dot(row_ref[0], wr)
    row = (row * sigm(row)).astype(BF16)
    row_out[...] = row
    corner_out[...] = row[-2 * SUB :]
    col = col_ref[:, SUB:, :].astype(F32)[:, SUB - 1, :].astype(BF16)
    col = dot(col, wr)
    col_out[...] = (col * sigm(col)).astype(BF16)


def turned(weight):
    return jnp.transpose(weight.astype(F32)).astype(BF16)


def weights_kernel(delta_ref, wr_ref, ws_ref, we_ref, sp_ref, wr_out, wp_out, wb_out, wt_out, wo_out):
    mid, cout = we_ref.shape
    wide = column(1.0 + delta_ref[...], mid)
    wr = wr_ref[...].astype(F32) * wide
    wr_out[...] = wr.astype(BF16)
    wo_out[...] = turned(wr)
    wp_out[:mid, :] = we_ref[...]
    wb_out[:, :mid] = turned(we_ref[...])
    for k in range(cout // mid):
        at = slice(k * mid, (k + 1) * mid)
        ws = ws_ref[:, at].astype(F32) * wide
        wp_out[mid:, at] = ws.astype(BF16)
        wb_out[at, mid:] = turned(ws)
    taps = (
        ((1, 1), (1, 2), (2, 1), (2, 2)),
        (None, (1, 0), None, (2, 0)),
        (None, None, (0, 1), (0, 2)),
        (None, None, None, (0, 0)),
    )
    for i, line in enumerate(taps):
        for j, tap in enumerate(line):
            value = jnp.zeros((mid, mid), BF16) if tap is None else turned(sp_ref[tap[0], tap[1]])
            wt_out[i * mid : (i + 1) * mid, j * mid : (j + 1) * mid] = value


def forward_kernel(
    tiles_r, tiles_c, x_ref, up_ref, corner_ref, left_ref, wr_ref, wc_ref, wp_ref, at_ref, as_ref, ao_ref, live_ref,
    slope1_ref, slope2_ref, slope3_ref, row2_ref, row3_ref, col2_ref, col3_ref,
    pay_ref, embed_ref, tval_ref, gval_ref, score_ref,
    red, lo, hi, taps, sums,
):
    step = pl.program_id(0)
    rows, cols, chan = x_ref.shape
    mid = wr_ref.shape[1]
    cout = wp_ref.shape[1]
    orow, ocol = rows // 2, cols // 2
    half = TILE // 2

    def put_taps(slot, source):
        for b, start in enumerate((SUB - 1, SUB, SUB + 1)):
            taps[slot, :, b * mid : (b + 1) * mid] = source[pl.ds(start, ocol, stride=2), :].astype(BF16)

    @pl.when(step == 0)
    def _():
        red[0, SUB - 1 : SUB, :] = corner_ref[...].astype(F32)[-1:]
        red[0, SUB:, :] = up_ref[...].astype(F32)
        put_taps(0, red.at[0])
        sums[...] = jnp.zeros_like(sums)

    @pl.when(step > 0)
    def _():
        taps[0] = taps[rows]

    pre = dot(x_ref[...].reshape(rows * cols, chan), wr_ref[...])
    sig = sigm(pre)
    act = pre * sig
    slope1_ref[...] = (sig + act * (1.0 - sig)).reshape(rows, cols, mid).astype(BF16)
    red[:, SUB:, :] = act.reshape(rows, cols, mid)
    left = left_ref[...].astype(F32)
    for r in range(rows):
        red[r, SUB - 1 : SUB, :] = left[r : r + 1]
        put_taps(r + 1, red.at[r])
    acc = jnp.zeros((orow * ocol, mid), F32)
    for a in range(3):
        part = jnp.stack([taps[2 * i + a] for i in range(orow)], axis=0)
        acc = acc + dot(part.reshape(orow * ocol, 3 * mid), wc_ref[a])
    sig = sigm(acc)
    act = acc * sig
    slope2 = (sig + act * (1.0 - sig)).reshape(orow, ocol, mid)
    slope2_ref[...] = slope2.astype(BF16)
    col2_ref[...] = slope2[:, 0, :]
    short = []
    for i in range(orow):
        lo[i] = x_ref[2 * i, :, : chan // 2].astype(F32)
        hi[i] = x_ref[2 * i, :, chan // 2 :].astype(F32)
    for i in range(orow):
        short.append(
            jnp.concatenate(
                [lo.at[i][pl.ds(0, ocol, stride=2), :].astype(BF16), hi.at[i][pl.ds(0, ocol, stride=2), :].astype(BF16)],
                axis=1,
            )
        )
    short = jnp.stack(short, axis=0).reshape(orow * ocol, chan)
    preact = dot(jnp.concatenate([act.astype(BF16), short], axis=1), wp_ref[...])
    sig = sigm(preact)
    act = preact * sig
    slope3 = (sig + act * (1.0 - sig)).reshape(orow, ocol, cout)
    slope3_ref[...] = slope3.astype(BF16)
    col3_ref[...] = slope3[:, 0, :]

    @pl.when(step == 0)
    def _():
        row2_ref[...] = slope2_ref[0]
        row3_ref[...] = slope3_ref[0]

    cells = jnp.sum(act.reshape(orow, tiles_c, half // SUB, SUB, cout), axis=(0, 2))
    trow = (step * orow) // half
    for c in range(tiles_c):
        slot = trow * tiles_c + c
        sums[slot] = sums[slot] + cells[c]

    @pl.when(step == pl.num_programs(0) - 1)
    def _():
        embed = jnp.sum(sums[...], axis=1) * (1.0 / (half * half))
        tval = jnp.tanh(jnp.dot(embed, at_ref[...], precision=HP, preferred_element_type=F32))
        gval = sigm(jnp.dot(embed, as_ref[...], precision=HP, preferred_element_type=F32))
        score = jnp.sum(tval * gval * ao_ref[...], axis=1, keepdims=True)
        live = live_ref[:, 0:1] > 0
        top = jnp.max(jnp.where(live, score, -1e30), axis=0, keepdims=True)
        weight = jnp.where(live, jnp.exp(score - top), 0.0)
        vector = jnp.sum(weight * embed, axis=0, keepdims=True)
        lines = cout // 128
        for k in range(lines):
            pay_ref[k : k + 1, :] = vector[:, k * 128 : (k + 1) * 128]
        pay_ref[lines : lines + 1, :] = jnp.broadcast_to(jnp.sum(weight, axis=0, keepdims=True), (1, 128))
        pay_ref[lines + 1 : lines + 2, :] = jnp.broadcast_to(top, (1, 128))
        pay_ref[lines + 2 :, :] = jnp.zeros((SUB - lines - 2, 128), F32)
        embed_ref[...] = embed
        tval_ref[...] = tval
        gval_ref[...] = gval
        score_ref[...] = jnp.broadcast_to(score, score_ref.shape)


AXES = ("head", "space")


def peer(sizes, k, hop):
    place = tuple(lax.axis_index(axis) for axis in AXES)
    other = lax.rem(place[k] + hop, sizes[k])
    return (other, place[1]) if k == 0 else (place[0], other)


def corner_of(sizes, hop):
    return tuple(lax.rem(lax.axis_index(axis) + n + hop, n) for axis, n in zip(AXES, sizes))


def greet(sizes, corners):
    barrier = pltpu.get_barrier_semaphore()
    count = 0
    for k in range(2):
        for hop in range(1, sizes[k]):
            pl.semaphore_signal(barrier, inc=1, device_id=peer(sizes, k, hop), device_id_type=MESH)
            count += 1
    if corners:
        for hop in (-1, 1):
            pl.semaphore_signal(barrier, inc=1, device_id=corner_of(sizes, hop), device_id_type=MESH)
            count += 1
    pl.semaphore_wait(barrier, count)


def exchanged(sizes, first, combine, rooms):
    got0, got1, mine, send0, send1, recv0, recv1 = rooms
    mine[0] = first
    for k in range(2):
        got, send, recv = (got0, got1)[k], (send0, send1)[k], (recv0, recv1)[k]
        copies = [
            pltpu.make_async_remote_copy(
                src_ref=mine.at[k],
                dst_ref=got.at[hop],
                send_sem=send.at[hop],
                recv_sem=recv.at[hop],
                device_id=peer(sizes, k, hop),
                device_id_type=MESH,
            )
            for hop in range(1, sizes[k])
        ]
        for copy in copies:
            copy.start()
        got[0] = mine[k]
        for copy in copies:
            copy.wait()
        result = combine(got[...])
        if k == 0:
            mine[1] = result
    return result


def exchange_rooms(sizes):
    shape = (SUB, 128)
    return [
        pltpu.VMEM((sizes[0],) + shape, F32),
        pltpu.VMEM((sizes[1],) + shape, F32),
        pltpu.VMEM((2,) + shape, F32),
        pltpu.SemaphoreType.DMA((sizes[0],)),
        pltpu.SemaphoreType.DMA((sizes[1],)),
        pltpu.SemaphoreType.DMA((sizes[0],)),
        pltpu.SemaphoreType.DMA((sizes[1],)),
    ]


def step_kernel(sizes, grad_ref, delta_ref, dir_ref, out_ref, *rooms):
    greet(sizes, False)
    chan = grad_ref.shape[1]
    lines = chan // 128
    part = jnp.sum(grad_ref[...], axis=0, keepdims=True)
    part = [part[:, k * 128 : (k + 1) * 128] for k in range(lines)]
    part = jnp.concatenate(part + [jnp.zeros((SUB - lines, 128), F32)], axis=0)
    total = exchanged(sizes, part, lambda every: jnp.sum(every, axis=0), rooms)
    delta = delta_ref[...]
    ddelta = jnp.concatenate([total[k : k + 1] for k in range(lines)], axis=1) / (1.0 + delta)
    norm = jnp.sqrt(jnp.sum(ddelta * ddelta, axis=1, keepdims=True) * (1.0 / chan) + 1e-06)
    out_ref[...] = delta + (2 * dir_ref[...] - 1).astype(F32) * float(ALPHA) * ddelta / norm


def spread(dembed_ref, first, tiles_c, half):
    cout = dembed_ref.shape[1]
    return jnp.concatenate(
        [jnp.broadcast_to(dembed_ref[pl.ds(first + c, 1), :], (half, cout)) for c in range(tiles_c)], axis=0
    )


def edge_kernel(
    sizes, tiles_r, tiles_c, pay_ref, embed_ref, tval_ref, gval_ref, score_ref, live_ref, ao_ref, cls_ref, at_ref, as_ref,
    wb_ref, row3_ref, row2_ref, col3_ref, col2_ref, dembed_ref, low_ref, right_ref,
    edges, landed, edge_send, edge_recv, *rooms,
):
    half = TILE // 2
    cout = embed_ref.shape[1]
    lines = cout // 128
    greet(sizes, True)

    def combine(every):
        top = jnp.max(every[:, lines + 1 : lines + 2, :], axis=0)
        factor = jnp.exp(every[:, lines + 1 : lines + 2, :] - top[None])
        total = jnp.sum(every[:, : lines + 1, :] * factor, axis=0)
        return jnp.concatenate([total, top, jnp.zeros((SUB - lines - 2, 128), F32)], axis=0)

    comb = exchanged(sizes, pay_ref[...], combine, rooms)
    total, top = comb[lines : lines + 1, 0:1], comb[lines + 1 : lines + 2, 0:1]
    pooled = jnp.concatenate([comb[k : k + 1] for k in range(lines)], axis=1) / total
    embed, tval, gval = embed_ref[...], tval_ref[...], gval_ref[...]
    ao, cls = ao_ref[...], cls_ref[...]
    live = live_ref[:, 0:1] > 0
    prob = jnp.where(live, jnp.exp(score_ref[:, 0:1] - top), 0.0) / total
    gap = jnp.sum(embed * cls, axis=1, keepdims=True) - jnp.sum(pooled * cls, axis=1, keepdims=True)
    datt = (prob * gap) * ao
    dtanh = datt * gval * (1.0 - tval * tval)
    dsigm = datt * tval * gval * (1.0 - gval)
    back = (((1,), (1,)), ((), ()))
    dembed = (
        prob * cls
        + lax.dot_general(dtanh, at_ref[...], back, precision=HP, preferred_element_type=F32)
        + lax.dot_general(dsigm, as_ref[...], back, precision=HP, preferred_element_type=F32)
    ) * (1.0 / (half * half))
    dembed_ref[...] = dembed
    ocol, mid = row2_ref.shape
    orow = col2_ref.shape[0]
    we = wb_ref[:, :mid]

    def spread_rows(rows):
        return jnp.concatenate([jnp.broadcast_to(dembed[t : t + 1], (half, cout)) for t in rows], axis=0)

    dpre = (row3_ref[...].astype(F32) * spread_rows(range(tiles_c))).astype(BF16)
    edges[0:ocol, :] = (dot(dpre, we) * row2_ref[...].astype(F32)).astype(BF16)
    dpre = (col3_ref[...] * spread_rows(range(0, tiles_r * tiles_c, tiles_c))).astype(BF16)
    edges[ocol : ocol + orow, :] = (dot(dpre, we) * col2_ref[...]).astype(BF16)
    spans = ((0, ocol, 0), (ocol, orow, ocol), (0, 2 * SUB, ocol + orow))
    targets = (peer(sizes, 1, sizes[1] - 1), peer(sizes, 0, sizes[0] - 1), corner_of(sizes, -1))
    copies = [
        pltpu.make_async_remote_copy(
            src_ref=edges.at[pl.ds(source, size)],
            dst_ref=landed.at[pl.ds(place, size)],
            send_sem=edge_send.at[k],
            recv_sem=edge_recv.at[k],
            device_id=targets[k],
            device_id_type=MESH,
        )
        for k, (source, size, place) in enumerate(spans)
    ]
    for copy in copies:
        copy.start()
    for copy in copies:
        copy.wait()
    inner = [lax.axis_index(axis) < n - 1 for axis, n in zip(AXES, sizes)]
    below = jnp.where(inner[1], 1.0, 0.0)
    beside = jnp.where(inner[0], 1.0, 0.0)
    low_ref[0:ocol, :] = landed[0:ocol, :].astype(F32) * below
    right_ref[...] = landed[ocol : ocol + orow, :].astype(F32) * beside
    low_ref[ocol:, :] = landed[ocol + orow :, :].astype(F32)[:SUB] * (below * beside)


def backward_kernel(
    tiles_c, x_ref, slope1_ref, slope2_ref, slope3_ref, dembed_ref, right_ref, low_ref, wb_ref, wt_ref, wo_ref,
    out_ref, grad_ref, dsx, drs, slo, shi,
):
    step = pl.program_id(0)
    rows, cols, chan = x_ref.shape
    orow, ocol, mid = slope2_ref.shape
    cout = slope3_ref.shape[2]
    half = TILE // 2
    block = pl.num_programs(0) - 1 - step
    trow = (block * orow) // half

    @pl.when(step == 0)
    def _():
        dsx[orow, :, :] = low_ref[...]
        slo[...] = jnp.zeros_like(slo)
        shi[...] = jnp.zeros_like(shi)
        grad_ref[...] = jnp.zeros_like(grad_ref)

    @pl.when(step > 0)
    def _():
        dsx[orow] = dsx[0]

    dpre = (slope3_ref[...].astype(F32) * spread(dembed_ref, trow * tiles_c, tiles_c, half)[None]).astype(BF16)
    both = dot(dpre.reshape(orow * ocol, cout), wb_ref[...])
    dsx[0:orow, 0:ocol, :] = both[:, :mid].reshape(orow, ocol, mid) * slope2_ref[...].astype(F32)
    for i in range(orow):
        dsx[i, ocol : ocol + 1, :] = right_ref[i : i + 1, :]
        slo[i, pl.ds(0, ocol, stride=2), :] = both[i * ocol : (i + 1) * ocol, mid : mid + chan // 2]
        shi[i, pl.ds(0, ocol, stride=2), :] = both[i * ocol : (i + 1) * ocol, mid + chan // 2 :]
    four = jnp.concatenate(
        [
            dsx[di : di + orow, dj : dj + ocol, :].astype(BF16).reshape(orow * ocol, mid)
            for di in range(2)
            for dj in range(2)
        ],
        axis=1,
    )
    grads = dot(four, wt_ref[...])
    for i in range(orow):
        for di in range(2):
            for dj in range(2):
                n = 2 * di + dj
                drs[2 * i + di, pl.ds(dj, ocol, stride=2), :] = grads[i * ocol : (i + 1) * ocol, n * mid : (n + 1) * mid]
    dred = (drs[...] * slope1_ref[...].astype(F32)).astype(BF16)
    dinput = dot(dred.reshape(rows * cols, mid), wo_ref[...]).reshape(rows, cols, chan)
    total = jnp.zeros((SUB, chan), F32)
    for r in range(rows):
        value = dinput[r]
        if r % 2 == 0:
            value = value + jnp.concatenate([slo[r // 2], shi[r // 2]], axis=1)
        out_ref[r] = value.astype(BF16)
        total = total + jnp.sum((value * x_ref[r].astype(F32)).reshape(cols // SUB, SUB, chan), axis=0)
    grad_ref[...] += total


def whole(shape):
    return pl.BlockSpec(shape, lambda i: (0,) * len(shape))


def shards(
    features,
    stain_delta,
    tissue,
    reduce_weight,
    spatial_weight,
    expand_weight,
    shortcut_weight,
    attn_tanh,
    attn_sigm,
    attn_out,
    classifier,
    step_dir,
):
    rows, cols, chan = features.shape
    mid = reduce_weight.shape[1]
    cout = expand_weight.shape[1]
    att = attn_out.shape[0]
    tiles_r, tiles_c = tissue.shape
    slots = -(-tiles_r * tiles_c // SUB) * SUB
    orow, ocol = rows // 2, cols // 2
    delta = stain_delta[None, :]
    wc = spatial_weight.reshape(3, 3 * mid, mid)
    live = jnp.pad((tissue.reshape(-1, 1) > 0).astype(F32), ((0, slots - tiles_r * tiles_c), (0, 127)))
    ao = attn_out[None, :]
    cls = classifier[None, :]
    sizes = tuple(lax.axis_size(axis) for axis in AXES)

    rim_row, rim_col, rim_corner = pl.pallas_call(
        rim_kernel,
        grid=(1,),
        out_shape=(
            jax.ShapeDtypeStruct((cols, mid), BF16),
            jax.ShapeDtypeStruct((rows, mid), BF16),
            jax.ShapeDtypeStruct((2 * SUB, mid), BF16),
        ),
        in_specs=[
            pl.BlockSpec((1, cols, chan), lambda i: (rows - 1, 0, 0)),
            pl.BlockSpec((rows, 2 * SUB, chan), lambda i: (0, cols // (2 * SUB) - 1, 0)),
            whole(delta.shape),
            whole(reduce_weight.shape),
        ],
        out_specs=(whole((cols, mid)), whole((rows, mid)), whole((2 * SUB, mid))),
        name="rim",
    )(features, features, delta, reduce_weight)
    up = passed_along(rim_row, "space", 1)
    left = passed_along(rim_col, "head", 1)
    corner = lax.ppermute(
        rim_corner,
        AXES,
        [
            (h * sizes[1] + s, (h + 1) * sizes[1] + s + 1)
            for h in range(sizes[0] - 1)
            for s in range(sizes[1] - 1)
        ],
    )
    wr, wp, wb, wt, wo = pl.pallas_call(
        weights_kernel,
        out_shape=(
            jax.ShapeDtypeStruct((chan, mid), BF16),
            jax.ShapeDtypeStruct((mid + chan, cout), BF16),
            jax.ShapeDtypeStruct((cout, mid + chan), BF16),
            jax.ShapeDtypeStruct((4 * mid, 4 * mid), BF16),
            jax.ShapeDtypeStruct((mid, chan), BF16),
        ),
        cost_estimate=pl.CostEstimate(flops=10**8, bytes_accessed=8 * 10**6, transcendentals=0),
        name="weights",
    )(delta, reduce_weight, shortcut_weight, expand_weight, spatial_weight)

    steps = rows // BLOCK
    params = pltpu.CompilerParams(dimension_semantics=("arbitrary",), vmem_limit_bytes=56 * 1024 * 1024)
    slope1, slope2, slope3, row2, row3, col2, col3, pay, embed, tval, gval, score = pl.pallas_call(
        functools.partial(forward_kernel, tiles_r, tiles_c),
        grid=(steps,),
        out_shape=(
            jax.ShapeDtypeStruct((rows, cols, mid), BF16),
            jax.ShapeDtypeStruct((orow, ocol, mid), BF16),
            jax.ShapeDtypeStruct((orow, ocol, cout), BF16),
            jax.ShapeDtypeStruct((ocol, mid), BF16),
            jax.ShapeDtypeStruct((ocol, cout), BF16),
            jax.ShapeDtypeStruct((orow, mid), F32),
            jax.ShapeDtypeStruct((orow, cout), F32),
            jax.ShapeDtypeStruct((SUB, 128), F32),
            jax.ShapeDtypeStruct((slots, cout), F32),
            jax.ShapeDtypeStruct((slots, att), F32),
            jax.ShapeDtypeStruct((slots, att), F32),
            jax.ShapeDtypeStruct((slots, 128), F32),
        ),
        in_specs=[
            pl.BlockSpec((BLOCK, cols, chan), lambda i: (i, 0, 0)),
            whole(up.shape),
            whole(corner.shape),
            pl.BlockSpec((BLOCK, mid), lambda i: (i, 0)),
            whole(wr.shape),
            whole(wc.shape),
            whole(wp.shape),
            whole(attn_tanh.shape),
            whole(attn_sigm.shape),
            whole(ao.shape),
            whole(live.shape),
        ],
        out_specs=(
            pl.BlockSpec((BLOCK, cols, mid), lambda i: (i, 0, 0)),
            pl.BlockSpec((BLOCK // 2, ocol, mid), lambda i: (i, 0, 0)),
            pl.BlockSpec((BLOCK // 2, ocol, cout), lambda i: (i, 0, 0)),
            whole((ocol, mid)),
            whole((ocol, cout)),
            pl.BlockSpec((BLOCK // 2, mid), lambda i: (i, 0)),
            pl.BlockSpec((BLOCK // 2, cout), lambda i: (i, 0)),
            whole((SUB, 128)),
            whole((slots, cout)),
            whole((slots, att)),
            whole((slots, att)),
            whole((slots, 128)),
        ),
        scratch_shapes=[
            pltpu.VMEM((BLOCK, cols + SUB, mid), F32),
            pltpu.VMEM((BLOCK // 2, cols, chan // 2), F32),
            pltpu.VMEM((BLOCK // 2, cols, chan // 2), F32),
            pltpu.VMEM((BLOCK + 1, ocol, 3 * mid), BF16),
            pltpu.VMEM((slots, SUB, cout), F32),
        ],
        compiler_params=params,
        name="forward",
    )(features, up, corner, left, wr, wc, wp, attn_tanh, attn_sigm, ao, live)

    dembed, low, right = pl.pallas_call(
        functools.partial(edge_kernel, sizes, tiles_r, tiles_c),
        out_shape=(
            jax.ShapeDtypeStruct((slots, cout), F32),
            jax.ShapeDtypeStruct((ocol + SUB, mid), F32),
            jax.ShapeDtypeStruct((orow, mid), F32),
        ),
        scratch_shapes=[
            pltpu.VMEM((ocol + orow, mid), BF16),
            pltpu.VMEM((ocol + orow + 2 * SUB, mid), BF16),
            pltpu.SemaphoreType.DMA((3,)),
            pltpu.SemaphoreType.DMA((3,)),
        ]
        + exchange_rooms(sizes),
        compiler_params=pltpu.CompilerParams(collective_id=0, has_side_effects=True),
        name="edge",
    )(pay, embed, tval, gval, score, live, ao, cls, attn_tanh, attn_sigm, wb, row3, row2, col3, col2)

    def turn(i):
        return (steps - 1 - i, 0, 0)

    feature_grad, partial_grad = pl.pallas_call(
        functools.partial(backward_kernel, tiles_c),
        grid=(steps,),
        out_shape=(
            jax.ShapeDtypeStruct((rows, cols, chan), BF16),
            jax.ShapeDtypeStruct((SUB, chan), F32),
        ),
        in_specs=[
            pl.BlockSpec((BLOCK, cols, chan), turn),
            pl.BlockSpec((BLOCK, cols, mid), turn),
            pl.BlockSpec((BLOCK // 2, ocol, mid), turn),
            pl.BlockSpec((BLOCK // 2, ocol, cout), turn),
            whole(dembed.shape),
            pl.BlockSpec((BLOCK // 2, mid), lambda i: (steps - 1 - i, 0)),
            whole(low.shape),
            whole(wb.shape),
            whole(wt.shape),
            whole(wo.shape),
        ],
        out_specs=(pl.BlockSpec((BLOCK, cols, chan), turn), whole((SUB, chan))),
        scratch_shapes=[
            pltpu.VMEM((BLOCK // 2 + 1, ocol + SUB, mid), F32),
            pltpu.VMEM((BLOCK, cols, mid), F32),
            pltpu.VMEM((BLOCK // 2, cols, chan // 2), F32),
            pltpu.VMEM((BLOCK // 2, cols, chan // 2), F32),
        ],
        compiler_params=params,
        name="backward",
    )(features, slope1, slope2, slope3, dembed, right, low, wb, wt, wo)

    new_delta = pl.pallas_call(
        functools.partial(step_kernel, sizes),
        out_shape=jax.ShapeDtypeStruct((1, chan), F32),
        scratch_shapes=exchange_rooms(sizes),
        compiler_params=pltpu.CompilerParams(collective_id=1, has_side_effects=True),
        name="step",
    )(partial_grad, delta, step_dir[None, :])[0]
    return (feature_grad, new_delta)


def solution(mesh):
    return jax.shard_map(
        shards,
        mesh=mesh,
        in_specs=(P("space", "head", None), P(), P("space", "head")) + (P(),) * 9,
        out_specs=(P("space", "head", None), P()),
        check_vma=False,
    )
```

time: 110 us -> 81.1 us (0.74)
  local copies, waits for them, and re-layouts: 23.5 us -> 1.92 us
  other arithmetic: 8.31 us -> 0.61 us
  waiting for transfers between devices: 4.76 us -> 0.01 us
  Pallas kernels: 61.8 us -> 66 us
  starting transfers between devices: 9.14 us -> 11.3 us
    pallas_call x2 -> x0, local copies, waits for them, and re-layouts: 8.48 us -> none  [shards(): pl.pallas_call(functools.partial(forward_kernel, tiles_r, tiles_c), grid=...]
    slice x11 -> x0, local copies, waits for them, and re-layouts: 6.18 us -> none  [the longest x1 1.46 us: shards(): slope3[:1]]
    ppermute x4 -> x2, waiting for transfers between devices: 4.76 us -> 0.01 us  [passed_along(): lax.ppermute(value, axis, [(source, source + steps) for source in range(f...]
    ppermute x0 -> x1, starting transfers between devices: none -> 4.27 us  [shards(): lax.ppermute(rim_corner, AXES, [(h * sizes[1] + s, (h + 1) * sizes[1] + s...]
    pallas_call x3 -> x4, Pallas kernels: 27.1 us -> 31 us  [the longest x1 15.9 us: shards(): pl.pallas_call(functools.partial(edge_kernel, sizes, tiles_r, tiles_c), o...]
    concatenate x7 -> x0, other arithmetic: 3.68 us -> none  [the longest x1 0.84 us: shards(): jnp.concatenate([jnp.concatenate([turned(1, 1), turned(1, 2), turned(2, 1...]
    squeeze x3 -> x0, local copies, waits for them, and re-layouts: 2.91 us -> none  [the longest x1 1.46 us: shards(): slope3[:, 0]]
    unnamed x21 -> x9, local copies, waits for them, and re-layouts: 4.14 us -> 1.83 us
  transfers between devices with their start and end apart: 4 -> 3, of which waited for: 2 -> 0; matrix products, arithmetic and copies ran while one was open for 9% -> 1% of each run, Pallas kernels for 0% -> 3%
where the time goes in v1:
time: 81.1 us; the launch traced here: 80.6 us
  Pallas kernels  66 us (81%)
  starting transfers between devices  11.3 us (14%)
  local copies, waits for them, and re-layouts  1.92 us (2%)
    pallas_call x1, Pallas kernels, shards(): pl.pallas_call(functools.partial(forward_kernel, tiles_r, tiles_c), grid=...  19.9 us
    pallas_call x1, Pallas kernels, shards(): pl.pallas_call(functools.partial(edge_kernel, sizes, tiles_r, tiles_c), o...  15.9 us
    pallas_call x1, Pallas kernels, shards(): pl.pallas_call(functools.partial(backward_kernel, tiles_c), grid=(steps,)...  15.2 us
    pallas_call x1, Pallas kernels, shards(): pl.pallas_call(functools.partial(step_kernel, sizes), out_shape=jax.Shape...  10.3 us
    ppermute x2, starting transfers between devices, passed_along(): lax.ppermute(value, axis, [(source, source + steps) for source in range(f...  6.99 us
    ppermute x1, starting transfers between devices, shards(): lax.ppermute(rim_corner, AXES, [(h * sizes[1] + s, (h + 1) * sizes[1] + s...  4.27 us
    pallas_call x1, Pallas kernels, shards(): pl.pallas_call(weights_kernel, out_shape=(jax.ShapeDtypeStruct((chan, mid...  2.51 us
    pallas_call x1, Pallas kernels, shards(): pl.pallas_call(rim_kernel, grid=(1,), out_shape=(jax.ShapeDtypeStruct((co...  2.25 us
  transfers between devices with their start and end apart: 3, of which 0 were waited for; matrix products, arithmetic and copies ran while one was open for 1% of the time, Pallas kernels for 3%

profile of v1, /device:TPU:0, one launch (start us, length us, event | category | flops | bytes accessed | tf_op | source)
XLA Modules:
  0.0 80.6 jit_solution(6663999320797302123)
XLA Ops:
  0.6 0.0 copy-start.3
  0.6 2.2 %rim.1 = (bf16[128,128]{1,0:T(8,128)(2,1)}, bf16[128,128]{1,0:T(8,128)(2,1)}, bf16[16,128]{1,0:T(8,128)(2,1)}) custom-call(bf16[128,128,256]{2,1,0:T(8,128)(2,1)} %x_ref.3, bf16[128,128,256]{2,1,0:T(8,128)(2,1)} %x_ref.3, f32[1,256]{1,0:T(1,128)} %bitcast.7, bf16[256,128]{1,0:T(8,128)(2,1)} %wr_ref.1), custom_call_target="tpu_custom_call" | custom-call | tf_op jit(solution)/shard_map/rim/pallas_call | solution.py:423
  2.9 4.3 %collective-permute-start.1 = (bf16[16,128]{1,0:T(8,128)(2,1)}, bf16[16,128]{1,0:T(8,128)(2,1)S(1)}, u32[]{:S(2)}, u32[]{:S(2)}) collective-permute-start(bf16[16,128]{1,0:T(8,128)(2,1)} %get-tuple-element.28), channel_id=1, source_target_pairs={{0,9},{1,10},{2,11},{3,12},{4,13},{5,14},{6,15},{8,17},{9,18},{10,... | collective-permute-start | bytes 12296 | tf_op jit(solution)/shard_map/ppermute | solution.py:442
  7.2 3.6 %collective-permute-start = (bf16[128,128]{1,0:T(8,128)(2,1)}, bf16[128,128]{1,0:T(8,128)(2,1)S(1)}, u32[]{:S(2)}, u32[]{:S(2)}) collective-permute-start(bf16[128,128]{1,0:T(8,128)(2,1)} %get-tuple-element.27), channel_id=1, source_target_pairs={{0,1},{1,2},{2,3},{3,4},{4,5},{5,6},{6,7},{8,9},{9,10},{10,11},{11... | collective-permute-start | bytes 98312 | tf_op jit(solution)/shard_map/ppermute | solution.py:27
  10.8 3.4 %collective-permute-start.2 = (bf16[128,128]{1,0:T(8,128)(2,1)}, bf16[128,128]{1,0:T(8,128)(2,1)S(1)}, u32[]{:S(2)}, u32[]{:S(2)}) collective-permute-start(bf16[128,128]{1,0:T(8,128)(2,1)} %get-tuple-element.29), channel_id=1, source_target_pairs={{0,8},{8,16},{16,24},{1,9},{9,17},{17,25},{2,10},{10,18},{18,26},{... | collective-permute-start | bytes 98312 | tf_op jit(solution)/shard_map/ppermute | solution.py:27
  14.2 0.0 copy-done.3
  14.2 0.1 convert_element_type.15
  14.3 0.6 pad_convert_fusion.live_ref
  14.9 2.5 %weights.1 = (bf16[256,128]{1,0:T(8,128)(2,1)}, bf16[384,512]{1,0:T(8,128)(2,1)}, bf16[512,384]{1,0:T(8,128)(2,1)}, bf16[512,512]{1,0:T(8,128)(2,1)}, bf16[128,256]{1,0:T(8,128)(2,1)}) custom-call(f32[1,256]{1,0:T(1,128)} %bitcast.8, bf16[256,128]{1,0:T(8,128)(2,1)} %wr_ref.1, bf16[256,512]{1,0:T(8,128)(2,1)} %ws_ref.1, bf16[128,512]{1,0:T(8,128)(2,1)} %we_ref.1, ...), custom_call_target="tpu_custom_call" | custom-call | flops 100000000 | bytes 8000000 | tf_op jit(solution)/shard_map/weights/pallas_call | solution.py:451
  17.4 0.0 collective-permute-done.1.corner_ref
  17.4 0.0 copy-start.2
  17.4 0.0 collective-permute-done.up_ref
  17.4 0.0 copy-start
  17.4 0.0 collective-permute-done.2.left_ref
  17.4 0.0 copy-start.1
  17.4 0.6 copy-done.2
  18.0 0.0 copy-done
  18.0 0.0 copy-done.1
  18.0 19.9 %forward.1 = (bf16[128,128,128]{2,1,0:T(8,128)(2,1)}, bf16[64,64,128]{2,1,0:T(8,128)(2,1)}, bf16[64,64,512]{2,1,0:T(8,128)(2,1)}, bf16[64,128]{1,0:T(8,128)(2,1)...) custom-call(bf16[128,128,256]{2,1,0:T(8,128)(2,1)} %x_ref.3, ...), custom_call_target="tpu_custom_call" | custom-call | tf_op jit(solution)/shard_map/forward/pallas_call | solution.py:466
  37.9 15.9 %edge.1 = (f32[8,512]{1,0:T(8,128)}, f32[72,128]{1,0:T(8,128)}, f32[64,128]{1,0:T(8,128)}) custom-call(f32[8,128]{1,0:T(8,128)} %get-tuple-element.35.pay_ref, f32[8,512]{1,0:T(8,128)} %get-tuple-element.36.embed_ref, f32[8,256]{1,0:T(8,128)} %get-tuple-element.37.tval_ref, f32[8,256]{1,0:T(8,128)} %get-tuple-element.38.gval_ref, ...), custom_call_target="tpu_custom_call" | custom-call | tf_op jit(solution)/shard_map/edge/pallas_call | solution.py:521
  53.8 15.2 %backward.1 = (bf16[128,128,256]{2,1,0:T(8,128)(2,1)}, f32[8,256]{1,0:T(8,128)}) custom-call(bf16[128,128,256]{2,1,0:T(8,128)(2,1)} %x_ref.3, bf16[128,128,128]{2,1,0:T(8,128)(2,1)} %get-tuple-element.32.slope1_ref, bf16[64,64,128]{2,1,0:T(8,128)(2,1)} %get-tuple-element.33.slope2_ref, bf16[64,64,512]{2,1,0:T(8,128)(2,1)} %get-tuple-element.34.slope3_ref, ...), custom_call_target="tpu_custom_call" | custom-call | tf_op jit(solution)/shard_map/backward/pallas_call | solution.py:542
  69.1 10.3 %step.1 = f32[1,256]{1,0:T(1,128)} custom-call(f32[8,256]{1,0:T(8,128)} %get-tuple-element.51.grad_ref, f32[1,256]{1,0:T(1,128)} %bitcast.9, s32[1,256]{1,0:T(1,128)} %bitcast.14), custom_call_target="tpu_custom_call" | custom-call | tf_op jit(solution)/shard_map/step/pallas_call | solution.py:572
  79.3 1.2 %copy.16 = f32[256]{0:T(256)} copy(f32[256]{0:T(256)} %bitcast.12) | data formatting | bytes 2048
  (1 shorter events, 0.0 us)
Async XLA Ops:
  0.6 13.5 %copy-start.3 = (s32[2,2]{1,0:T(2,128)S(1)}, s32[2,2]{1,0:T(2,128)}, u32[]{:S(2)}) copy-start(s32[2,2]{1,0:T(2,128)} %param.14) | copy-start | bytes 52
  2.9 14.5 %collective-permute-start.1 = (bf16[16,128]{1,0:T(8,128)(2,1)}, bf16[16,128]{1,0:T(8,128)(2,1)S(1)}, u32[]{:S(2)}, u32[]{:S(2)}) collective-permute-start(bf16[16,128]{1,0:T(8,128)(2,1)} %get-tuple-element.28), channel_id=1, source_target_pairs={{0,9},{1,10},{2,11},{3,12},{4,13},{5,14},{6,15},{8,17},{9,18},{10,... | collective-permute-start | bytes 12296 | tf_op jit(solution)/shard_map/ppermute | solution.py:442
  7.2 10.2 %collective-permute-start = (bf16[128,128]{1,0:T(8,128)(2,1)}, bf16[128,128]{1,0:T(8,128)(2,1)S(1)}, u32[]{:S(2)}, u32[]{:S(2)}) collective-permute-start(bf16[128,128]{1,0:T(8,128)(2,1)} %get-tuple-element.27), channel_id=1, source_target_pairs={{0,1},{1,2},{2,3},{3,4},{4,5},{5,6},{6,7},{8,9},{9,10},{10,11},{11... | collective-permute-start | bytes 98312 | tf_op jit(solution)/shard_map/ppermute | solution.py:27
  10.8 6.7 %collective-permute-start.2 = (bf16[128,128]{1,0:T(8,128)(2,1)}, bf16[128,128]{1,0:T(8,128)(2,1)S(1)}, u32[]{:S(2)}, u32[]{:S(2)}) collective-permute-start(bf16[128,128]{1,0:T(8,128)(2,1)} %get-tuple-element.29), channel_id=1, source_target_pairs={{0,8},{8,16},{16,24},{1,9},{9,17},{17,25},{2,10},{10,18},{18,26},{... | collective-permute-start | bytes 98312 | tf_op jit(solution)/shard_map/ppermute | solution.py:27
  17.4 0.6 copy-start.2
  17.4 0.6 copy-start
  17.4 0.6 copy-start.1

commit v2 on v1

--- a/solution.py
+++ b/solution.py
@@ -9,7 +9,7 @@
 
 TILE = 64
 ALPHA = 1
-BLOCK = 16
+BLOCK = 32
 SUB = 8
 F32 = jnp.float32
 MESH = pl.DeviceIdType.MESH
@@ -21,12 +21,6 @@
     return 0.5 + 0.5 * jnp.tanh(0.5 * value)
 
 
-def passed_along(value, axis, steps):
-    count = lax.axis_size(axis)
-    first, last = (max(0, -steps), min(count, count - steps))
-    return lax.ppermute(value, axis, [(source, source + steps) for source in range(first, last)])
-
-
 def dot(a, b):
     return jnp.dot(a, b, preferred_element_type=F32)
 
@@ -35,49 +29,12 @@
     return jnp.transpose(jnp.broadcast_to(row, (width, row.shape[1])))
 
 
-def rim_kernel(row_ref, col_ref, delta_ref, w_ref, row_out, col_out, corner_out):
-    mid = w_ref.shape[1]
-    wr = (w_ref[...].astype(F32) * column(1.0 + delta_ref[...], mid)).astype(BF16)
-    row = dot(row_ref[0], wr)
-    row = (row * sigm(row)).astype(BF16)
-    row_out[...] = row
-    corner_out[...] = row[-2 * SUB :]
-    col = col_ref[:, SUB:, :].astype(F32)[:, SUB - 1, :].astype(BF16)
-    col = dot(col, wr)
-    col_out[...] = (col * sigm(col)).astype(BF16)
-
-
 def turned(weight):
     return jnp.transpose(weight.astype(F32)).astype(BF16)
 
 
-def weights_kernel(delta_ref, wr_ref, ws_ref, we_ref, sp_ref, wr_out, wp_out, wb_out, wt_out, wo_out):
-    mid, cout = we_ref.shape
-    wide = column(1.0 + delta_ref[...], mid)
-    wr = wr_ref[...].astype(F32) * wide
-    wr_out[...] = wr.astype(BF16)
-    wo_out[...] = turned(wr)
-    wp_out[:mid, :] = we_ref[...]
-    wb_out[:, :mid] = turned(we_ref[...])
-    for k in range(cout // mid):
-        at = slice(k * mid, (k + 1) * mid)
-        ws = ws_ref[:, at].astype(F32) * wide
-        wp_out[mid:, at] = ws.astype(BF16)
-        wb_out[at, mid:] = turned(ws)
-    taps = (
-        ((1, 1), (1, 2), (2, 1), (2, 2)),
-        (None, (1, 0), None, (2, 0)),
-        (None, None, (0, 1), (0, 2)),
-        (None, None, None, (0, 0)),
-    )
-    for i, line in enumerate(taps):
-        for j, tap in enumerate(line):
-            value = jnp.zeros((mid, mid), BF16) if tap is None else turned(sp_ref[tap[0], tap[1]])
-            wt_out[i * mid : (i + 1) * mid, j * mid : (j + 1) * mid] = value
-
-
 def forward_kernel(
-    tiles_r, tiles_c, x_ref, up_ref, corner_ref, left_ref, wr_ref, wc_ref, wp_ref, at_ref, as_ref, ao_ref, live_ref,
+    tiles_r, tiles_c, x_ref, up_ref, left_ref, wr_ref, wc_ref, wp_ref, at_ref, as_ref, ao_ref, live_ref,
     slope1_ref, slope2_ref, slope3_ref, row2_ref, row3_ref, col2_ref, col3_ref,
     pay_ref, embed_ref, tval_ref, gval_ref, score_ref,
     red, lo, hi, taps, sums,
@@ -95,9 +52,7 @@
 
     @pl.when(step == 0)
     def _():
-        red[0, SUB - 1 : SUB, :] = corner_ref[...].astype(F32)[-1:]
-        red[0, SUB:, :] = up_ref[...].astype(F32)
-        put_taps(0, red.at[0])
+        put_taps(0, up_ref)
         sums[...] = jnp.zeros_like(sums)
 
     @pl.when(step > 0)
@@ -109,9 +64,8 @@
     act = pre * sig
     slope1_ref[...] = (sig + act * (1.0 - sig)).reshape(rows, cols, mid).astype(BF16)
     red[:, SUB:, :] = act.reshape(rows, cols, mid)
-    left = left_ref[...].astype(F32)
     for r in range(rows):
-        red[r, SUB - 1 : SUB, :] = left[r : r + 1]
+        red[r, SUB - 1 : SUB, :] = left_ref[r : r + 1, :]
         put_taps(r + 1, red.at[r])
     acc = jnp.zeros((orow * ocol, mid), F32)
     for a in range(3):
@@ -171,7 +125,7 @@
         embed_ref[...] = embed
         tval_ref[...] = tval
         gval_ref[...] = gval
-        score_ref[...] = jnp.broadcast_to(score, score_ref.shape)
+        score_ref[...] = jnp.where(live, jnp.broadcast_to(score, score_ref.shape), -1e30)
 
 
 AXES = ("head", "space")
@@ -241,6 +195,66 @@
     ]
 
 
+def rim_kernel(
+    sizes, row_ref, col_ref, delta_ref, wr_ref, ws_ref, we_ref, sp_ref,
+    up_out, left_out, wr_out, wp_out, wb_out, wt_out, wo_out,
+    edges, landed, edge_send, edge_recv,
+):
+    targets = (peer(sizes, 1, 1), peer(sizes, 0, 1), corner_of(sizes, 1))
+    sources = (peer(sizes, 1, sizes[1] - 1), peer(sizes, 0, sizes[0] - 1), corner_of(sizes, -1))
+    barrier = pltpu.get_barrier_semaphore()
+    for device in targets + sources:
+        pl.semaphore_signal(barrier, inc=1, device_id=device, device_id_type=MESH)
+    mid, cout = we_ref.shape
+    cols, rows = row_ref.shape[1], col_ref.shape[0]
+    wide = column(1.0 + delta_ref[...], mid)
+    wr = wr_ref[...].astype(F32) * wide
+    wr_out[...] = wr.astype(BF16)
+    col = col_ref[:, SUB:, :].astype(F32)[:, SUB - 1, :].astype(BF16)
+    both = dot(jnp.concatenate([row_ref[0], col], axis=0), wr.astype(BF16))
+    edges[...] = (both * sigm(both)).astype(BF16)
+    spans = ((0, cols, 0), (cols, rows, cols), (cols - 2 * SUB, 2 * SUB, cols + rows))
+    copies = [
+        pltpu.make_async_remote_copy(
+            src_ref=edges.at[pl.ds(source, size)],
+            dst_ref=landed.at[pl.ds(place, size)],
+            send_sem=edge_send.at[k],
+            recv_sem=edge_recv.at[k],
+            device_id=targets[k],
+            device_id_type=MESH,
+        )
+        for k, (source, size, place) in enumerate(spans)
+    ]
+    pl.semaphore_wait(barrier, 6)
+    for copy in copies:
+        copy.start()
+    wo_out[...] = turned(wr)
+    wp_out[:mid, :] = we_ref[...]
+    wb_out[:, :mid] = turned(we_ref[...])
+    for k in range(cout // mid):
+        at = slice(k * mid, (k + 1) * mid)
+        ws = ws_ref[:, at].astype(F32) * wide
+        wp_out[mid:, at] = ws.astype(BF16)
+        wb_out[at, mid:] = turned(ws)
+    taps = (
+        ((1, 1), (1, 2), (2, 1), (2, 2)),
+        (None, (1, 0), None, (2, 0)),
+        (None, None, (0, 1), (0, 2)),
+        (None, None, None, (0, 0)),
+    )
+    for i, line in enumerate(taps):
+        for j, tap in enumerate(line):
+            value = jnp.zeros((mid, mid), BF16) if tap is None else turned(sp_ref[tap[0], tap[1]])
+            wt_out[i * mid : (i + 1) * mid, j * mid : (j + 1) * mid] = value
+    for copy in copies:
+        copy.wait()
+    above = jnp.where(lax.axis_index("space") > 0, 1.0, 0.0)
+    beside = jnp.where(lax.axis_index("head") > 0, 1.0, 0.0)
+    up_out[0:SUB, :] = landed[cols + rows :, :].astype(F32)[SUB:] * (above * beside)
+    up_out[SUB:, :] = landed[0:cols, :].astype(F32) * above
+    left_out[...] = landed[cols : cols + rows, :].astype(F32) * beside
+
+
 def step_kernel(sizes, grad_ref, delta_ref, dir_ref, out_ref, *rooms):
     greet(sizes, False)
     chan = grad_ref.shape[1]
@@ -252,7 +266,7 @@
     delta = delta_ref[...]
     ddelta = jnp.concatenate([total[k : k + 1] for k in range(lines)], axis=1) / (1.0 + delta)
     norm = jnp.sqrt(jnp.sum(ddelta * ddelta, axis=1, keepdims=True) * (1.0 / chan) + 1e-06)
-    out_ref[...] = delta + (2 * dir_ref[...] - 1).astype(F32) * float(ALPHA) * ddelta / norm
+    out_ref[...] = (2 * dir_ref[...] - 1).astype(F32) * float(ALPHA) * ddelta / norm
 
 
 def spread(dembed_ref, first, tiles_c, half):
@@ -420,46 +434,45 @@
     cls = classifier[None, :]
     sizes = tuple(lax.axis_size(axis) for axis in AXES)
 
-    rim_row, rim_col, rim_corner = pl.pallas_call(
-        rim_kernel,
+    up, left, wr, wp, wb, wt, wo = pl.pallas_call(
+        functools.partial(rim_kernel, sizes),
         grid=(1,),
         out_shape=(
-            jax.ShapeDtypeStruct((cols, mid), BF16),
-            jax.ShapeDtypeStruct((rows, mid), BF16),
-            jax.ShapeDtypeStruct((2 * SUB, mid), BF16),
+            jax.ShapeDtypeStruct((cols + SUB, mid), F32),
+            jax.ShapeDtypeStruct((rows, mid), F32),
+            jax.ShapeDtypeStruct((chan, mid), BF16),
+            jax.ShapeDtypeStruct((mid + chan, cout), BF16),
+            jax.ShapeDtypeStruct((cout, mid + chan), BF16),
+            jax.ShapeDtypeStruct((4 * mid, 4 * mid), BF16),
+            jax.ShapeDtypeStruct((mid, chan), BF16),
         ),
         in_specs=[
             pl.BlockSpec((1, cols, chan), lambda i: (rows - 1, 0, 0)),
             pl.BlockSpec((rows, 2 * SUB, chan), lambda i: (0, cols // (2 * SUB) - 1, 0)),
             whole(delta.shape),
             whole(reduce_weight.shape),
+            whole(shortcut_weight.shape),
+            whole(expand_weight.shape),
+            whole(spatial_weight.shape),
         ],
-        out_specs=(whole((cols, mid)), whole((rows, mid)), whole((2 * SUB, mid))),
+        out_specs=(
+            whole((cols + SUB, mid)),
+            whole((rows, mid)),
+            whole((chan, mid)),
+            whole((mid + chan, cout)),
+            whole((cout, mid + chan)),
+            whole((4 * mid, 4 * mid)),
+            whole((mid, chan)),
+        ),
+        scratch_shapes=[
+            pltpu.VMEM((cols + rows, mid), BF16),
+            pltpu.VMEM((cols + rows + 2 * SUB, mid), BF16),
+            pltpu.SemaphoreType.DMA((3,)),
+            pltpu.SemaphoreType.DMA((3,)),
+        ],
+        compiler_params=pltpu.CompilerParams(collective_id=2, has_side_effects=True),
         name="rim",
-    )(features, features, delta, reduce_weight)
-    up = passed_along(rim_row, "space", 1)
-    left = passed_along(rim_col, "head", 1)
-    corner = lax.ppermute(
-        rim_corner,
-        AXES,
-        [
-            (h * sizes[1] + s, (h + 1) * sizes[1] + s + 1)
-            for h in range(sizes[0] - 1)
-            for s in range(sizes[1] - 1)
-        ],
-    )
-    wr, wp, wb, wt, wo = pl.pallas_call(
-        weights_kernel,
-        out_shape=(
-            jax.ShapeDtypeStruct((chan, mid), BF16),
-            jax.ShapeDtypeStruct((mid + chan, cout), BF16),
-            jax.ShapeDtypeStruct((cout, mid + chan), BF16),
-            jax.ShapeDtypeStruct((4 * mid, 4 * mid), BF16),
-            jax.ShapeDtypeStruct((mid, chan), BF16),
-        ),
-        cost_estimate=pl.CostEstimate(flops=10**8, bytes_accessed=8 * 10**6, transcendentals=0),
-        name="weights",
-    )(delta, reduce_weight, shortcut_weight, expand_weight, spatial_weight)
+    )(features, features, delta, reduce_weight, shortcut_weight, expand_weight, spatial_weight)
 
     steps = rows // BLOCK
     params = pltpu.CompilerParams(dimension_semantics=("arbitrary",), vmem_limit_bytes=56 * 1024 * 1024)
@@ -483,7 +496,6 @@
         in_specs=[
             pl.BlockSpec((BLOCK, cols, chan), lambda i: (i, 0, 0)),
             whole(up.shape),
-            whole(corner.shape),
             pl.BlockSpec((BLOCK, mid), lambda i: (i, 0)),
             whole(wr.shape),
             whole(wc.shape),
@@ -516,7 +528,7 @@
         ],
         compiler_params=params,
         name="forward",
-    )(features, up, corner, left, wr, wc, wp, attn_tanh, attn_sigm, ao, live)
+    )(features, up, left, wr, wc, wp, attn_tanh, attn_sigm, ao, live)
 
     dembed, low, right = pl.pallas_call(
         functools.partial(edge_kernel, sizes, tiles_r, tiles_c),
@@ -569,7 +581,7 @@
         name="backward",
     )(features, slope1, slope2, slope3, dembed, right, low, wb, wt, wo)
 
-    new_delta = pl.pallas_call(
+    new_delta = stain_delta + pl.pallas_call(
         functools.partial(step_kernel, sizes),
         out_shape=jax.ShapeDtypeStruct((1, chan), F32),
         scratch_shapes=exchange_rooms(sizes),

time: 81.1 us -> 72.8 us (0.90)
  starting transfers between devices: 11.3 us -> 0 us
  Pallas kernels: 66 us -> 69.3 us
  other arithmetic: 0.61 us -> 2.48 us
  local copies, waits for them, and re-layouts: 1.92 us -> 0.09 us
    ppermute x3 -> x0, starting transfers between devices: 11.3 us -> none  [the longest x2 6.99 us: passed_along(): lax.ppermute(value, axis, [(source, source + steps) for source in range(f...]
    pallas_call x2 -> x1, Pallas kernels: 4.76 us -> 11.6 us  [shards(): pl.pallas_call(functools.partial(rim_kernel, sizes), grid=(1,), out_shape...]
    unnamed x9 -> x2, local copies, waits for them, and re-layouts: 1.83 us -> 0.01 us
    pallas_call x1, Pallas kernels: 19.9 us -> 18.3 us  [shards(): pl.pallas_call(functools.partial(forward_kernel, tiles_r, tiles_c), grid=...]
    pallas_call x1, Pallas kernels: 15.2 us -> 13.9 us  [shards(): pl.pallas_call(functools.partial(backward_kernel, tiles_c), grid=(steps,)...]
    add x0 -> x1, other arithmetic: none -> 1.2 us  [shards(): stain_delta + pl.pallas_call(functools.partial(step_kernel, sizes), out_s...]
    pallas_call x1, Pallas kernels: 15.9 us -> 15 us  [shards(): pl.pallas_call(functools.partial(edge_kernel, sizes, tiles_r, tiles_c), o...]
  transfers between devices with their start and end apart: 3 -> 0, of which waited for: 0 -> 0; matrix products, arithmetic and copies ran while one was open for 1% -> 0% of each run, Pallas kernels for 3% -> 0%
where the time goes in v2:
time: 72.8 us; the launch traced here: 72.5 us
  Pallas kernels  69.3 us (95%)
  other arithmetic  2.48 us (3%)
    pallas_call x1, Pallas kernels, shards(): pl.pallas_call(functools.partial(forward_kernel, tiles_r, tiles_c), grid=...  18.3 us
    pallas_call x1, Pallas kernels, shards(): pl.pallas_call(functools.partial(edge_kernel, sizes, tiles_r, tiles_c), o...  15 us
    pallas_call x1, Pallas kernels, shards(): pl.pallas_call(functools.partial(backward_kernel, tiles_c), grid=(steps,)...  13.9 us
    pallas_call x1, Pallas kernels, shards(): pl.pallas_call(functools.partial(rim_kernel, sizes), grid=(1,), out_shape...  11.6 us
    pallas_call x1, Pallas kernels, shards(): pl.pallas_call(functools.partial(step_kernel, sizes), out_shape=jax.Shape...  10.5 us

profile of v2, /device:TPU:0, one launch (start us, length us, event | category | flops | bytes accessed | tf_op | source)
XLA Modules:
  0.0 72.5 jit_solution(11380591777978380441)
XLA Ops:
  0.6 0.7 broadcast_compare_fusion
  1.3 0.1 convert_element_type.15
  1.4 0.6 pad_convert_fusion.live_ref
  2.0 11.6 %rim.1 = (f32[136,128]{1,0:T(8,128)}, f32[128,128]{1,0:T(8,128)}, bf16[256,128]{1,0:T(8,128)(2,1)}, bf16[384,512]{1,0:T(8,128)(2,1)}, bf16[512,384]{1,0:T(8,128)...) custom-call(bf16[128,128,256]{2,1,0:T(8,128)(2,1)} %x_ref.3, bf16[128,128,256]{2,1,0:T(8,128)(2,1)} %x_ref.3, ...), custom_call_target="tpu_custom_call" | custom-call | tf_op jit(solution)/shard_map/rim/pallas_call | solution.py:437
  13.6 18.3 %forward.1 = (bf16[128,128,128]{2,1,0:T(8,128)(2,1)}, bf16[64,64,128]{2,1,0:T(8,128)(2,1)}, bf16[64,64,512]{2,1,0:T(8,128)(2,1)}, bf16[64,128]{1,0:T(8,128)(2,1)...) custom-call(bf16[128,128,256]{2,1,0:T(8,128)(2,1)} %x_ref.3, ...), custom_call_target="tpu_custom_call" | custom-call | tf_op jit(solution)/shard_map/forward/pallas_call | solution.py:479
  32.0 15.0 %edge.1 = (f32[8,512]{1,0:T(8,128)}, f32[72,128]{1,0:T(8,128)}, f32[64,128]{1,0:T(8,128)}) custom-call(f32[8,128]{1,0:T(8,128)} %get-tuple-element.33.pay_ref, f32[8,512]{1,0:T(8,128)} %get-tuple-element.34.embed_ref, f32[8,256]{1,0:T(8,128)} %get-tuple-element.35.tval_ref, f32[8,256]{1,0:T(8,128)} %get-tuple-element.36.gval_ref, ...), custom_call_target="tpu_custom_call" | custom-call | tf_op jit(solution)/shard_map/edge/pallas_call | solution.py:533
  46.9 0.0 copy-start
  47.0 13.9 %backward.1 = (bf16[128,128,256]{2,1,0:T(8,128)(2,1)}, f32[8,256]{1,0:T(8,128)}) custom-call(bf16[128,128,256]{2,1,0:T(8,128)(2,1)} %x_ref.3, bf16[128,128,128]{2,1,0:T(8,128)(2,1)} %get-tuple-element.30.slope1_ref, bf16[64,64,128]{2,1,0:T(8,128)(2,1)} %get-tuple-element.31.slope2_ref, bf16[64,64,512]{2,1,0:T(8,128)(2,1)} %get-tuple-element.32.slope3_ref, ...), custom_call_target="tpu_custom_call" | custom-call | tf_op jit(solution)/shard_map/backward/pallas_call | solution.py:554
  60.8 10.5 %step.1 = f32[1,256]{1,0:T(1,128)} custom-call(f32[8,256]{1,0:T(8,128)} %get-tuple-element.49.grad_ref, f32[1,256]{1,0:T(1,128)} %bitcast.8, s32[1,256]{1,0:T(1,128)} %bitcast.13), custom_call_target="tpu_custom_call" | custom-call | tf_op jit(solution)/shard_map/step/pallas_call | solution.py:584
  71.3 0.0 copy-done
  71.3 1.2 %add.3 = f32[256]{0:T(256)} add(f32[256]{0:T(256)S(1)} %copy-done, f32[256]{0:T(256)} %bitcast.11) | non-fusion elementwise | flops 256 | bytes 3072 | tf_op jit(solution)/shard_map/add | solution.py:584
Async XLA Ops:
  46.9 24.4 %copy-start = (f32[256]{0:T(256)S(1)}, f32[256]{0:T(256)}, u32[]{:S(2)}) copy-start(f32[256]{0:T(256)} %param.13) | copy-start | bytes 3076

commit v3 on v2

--- a/solution.py
+++ b/solution.py
@@ -34,10 +34,9 @@
 
 
 def forward_kernel(
-    tiles_r, tiles_c, x_ref, up_ref, left_ref, wr_ref, wc_ref, wp_ref, at_ref, as_ref, ao_ref, live_ref,
-    slope1_ref, slope2_ref, slope3_ref, row2_ref, row3_ref, col2_ref, col3_ref,
-    pay_ref, embed_ref, tval_ref, gval_ref, score_ref,
-    red, lo, hi, taps, sums,
+    sizes, x_ref, up_ref, left_ref, wr_ref, wc_ref, wp_ref, at_ref, as_ref, ao_ref, cls_ref, wb_ref, tissue_ref,
+    slope1_ref, slope2_ref, slope3_ref, dembed_ref, low_ref, right_ref,
+    red, lo, hi, taps, sums, row2, row3, col2, col3, *edge_rooms,
 ):
     step = pl.program_id(0)
     rows, cols, chan = x_ref.shape
@@ -45,6 +44,7 @@
     cout = wp_ref.shape[1]
     orow, ocol = rows // 2, cols // 2
     half = TILE // 2
+    tiles_r, tiles_c = tissue_ref.shape
 
     def put_taps(slot, source):
         for b, start in enumerate((SUB - 1, SUB, SUB + 1)):
@@ -52,6 +52,7 @@
 
     @pl.when(step == 0)
     def _():
+        greet(sizes, True)
         put_taps(0, up_ref)
         sums[...] = jnp.zeros_like(sums)
 
@@ -75,7 +76,7 @@
     act = acc * sig
     slope2 = (sig + act * (1.0 - sig)).reshape(orow, ocol, mid)
     slope2_ref[...] = slope2.astype(BF16)
-    col2_ref[...] = slope2[:, 0, :]
+    col2[pl.ds(pl.multiple_of(step * orow, orow), orow), :] = slope2[:, 0, :]
     short = []
     for i in range(orow):
         lo[i] = x_ref[2 * i, :, : chan // 2].astype(F32)
@@ -93,12 +94,12 @@
     act = preact * sig
     slope3 = (sig + act * (1.0 - sig)).reshape(orow, ocol, cout)
     slope3_ref[...] = slope3.astype(BF16)
-    col3_ref[...] = slope3[:, 0, :]
+    col3[pl.ds(pl.multiple_of(step * orow, orow), orow), :] = slope3[:, 0, :]
 
     @pl.when(step == 0)
     def _():
-        row2_ref[...] = slope2_ref[0]
-        row3_ref[...] = slope3_ref[0]
+        row2[...] = slope2_ref[0]
+        row3[...] = slope3_ref[0]
 
     cells = jnp.sum(act.reshape(orow, tiles_c, half // SUB, SUB, cout), axis=(0, 2))
     trow = (step * orow) // half
@@ -108,24 +109,10 @@
 
     @pl.when(step == pl.num_programs(0) - 1)
     def _():
-        embed = jnp.sum(sums[...], axis=1) * (1.0 / (half * half))
-        tval = jnp.tanh(jnp.dot(embed, at_ref[...], precision=HP, preferred_element_type=F32))
-        gval = sigm(jnp.dot(embed, as_ref[...], precision=HP, preferred_element_type=F32))
-        score = jnp.sum(tval * gval * ao_ref[...], axis=1, keepdims=True)
-        live = live_ref[:, 0:1] > 0
-        top = jnp.max(jnp.where(live, score, -1e30), axis=0, keepdims=True)
-        weight = jnp.where(live, jnp.exp(score - top), 0.0)
-        vector = jnp.sum(weight * embed, axis=0, keepdims=True)
-        lines = cout // 128
-        for k in range(lines):
-            pay_ref[k : k + 1, :] = vector[:, k * 128 : (k + 1) * 128]
-        pay_ref[lines : lines + 1, :] = jnp.broadcast_to(jnp.sum(weight, axis=0, keepdims=True), (1, 128))
-        pay_ref[lines + 1 : lines + 2, :] = jnp.broadcast_to(top, (1, 128))
-        pay_ref[lines + 2 :, :] = jnp.zeros((SUB - lines - 2, 128), F32)
-        embed_ref[...] = embed
-        tval_ref[...] = tval
-        gval_ref[...] = gval
-        score_ref[...] = jnp.where(live, jnp.broadcast_to(score, score_ref.shape), -1e30)
+        finish(
+            sizes, tiles_r, tiles_c, sums, at_ref, as_ref, ao_ref, cls_ref, wb_ref, tissue_ref, row2, row3, col2, col3,
+            dembed_ref, low_ref, right_ref, *edge_rooms,
+        )
 
 
 AXES = ("head", "space")
@@ -143,16 +130,16 @@
 
 def greet(sizes, corners):
     barrier = pltpu.get_barrier_semaphore()
-    count = 0
     for k in range(2):
         for hop in range(1, sizes[k]):
             pl.semaphore_signal(barrier, inc=1, device_id=peer(sizes, k, hop), device_id_type=MESH)
-            count += 1
     if corners:
         for hop in (-1, 1):
             pl.semaphore_signal(barrier, inc=1, device_id=corner_of(sizes, hop), device_id_type=MESH)
-            count += 1
-    pl.semaphore_wait(barrier, count)
+
+
+def wait_greetings(sizes, corners):
+    pl.semaphore_wait(pltpu.get_barrier_semaphore(), sizes[0] + sizes[1] - 2 + (2 if corners else 0))
 
 
 def exchanged(sizes, first, combine, rooms):
@@ -257,6 +244,7 @@
 
 def step_kernel(sizes, grad_ref, delta_ref, dir_ref, out_ref, *rooms):
     greet(sizes, False)
+    wait_greetings(sizes, False)
     chan = grad_ref.shape[1]
     lines = chan // 128
     part = jnp.sum(grad_ref[...], axis=0, keepdims=True)
@@ -276,15 +264,37 @@
     )
 
 
-def edge_kernel(
-    sizes, tiles_r, tiles_c, pay_ref, embed_ref, tval_ref, gval_ref, score_ref, live_ref, ao_ref, cls_ref, at_ref, as_ref,
-    wb_ref, row3_ref, row2_ref, col3_ref, col2_ref, dembed_ref, low_ref, right_ref,
-    edges, landed, edge_send, edge_recv, *rooms,
+def finish(
+    sizes, tiles_r, tiles_c, sums, at_ref, as_ref, ao_ref, cls_ref, wb_ref, tissue_ref, row2, row3, col2, col3,
+    dembed_ref, low_ref, right_ref, edges, landed, edge_send, edge_recv, *rooms,
 ):
     half = TILE // 2
-    cout = embed_ref.shape[1]
+    cout = cls_ref.shape[1]
     lines = cout // 128
-    greet(sizes, True)
+    ao, cls = ao_ref[...], cls_ref[...]
+    embed = jnp.sum(sums[...], axis=1) * (1.0 / (half * half))
+    tval = jnp.tanh(jnp.dot(embed, at_ref[...], precision=HP, preferred_element_type=F32))
+    gval = sigm(jnp.dot(embed, as_ref[...], precision=HP, preferred_element_type=F32))
+    score = jnp.sum(tval * gval * ao, axis=1, keepdims=True)
+    slot = lax.broadcasted_iota(jnp.int32, (embed.shape[0], 128), 0)
+    marks = jnp.zeros(slot.shape, jnp.int32)
+    for r in range(tiles_r):
+        for c in range(tiles_c):
+            mark = jnp.broadcast_to(tissue_ref[r : r + 1, c : c + 1], slot.shape)
+            marks = jnp.where(slot == r * tiles_c + c, mark, marks)
+    live = marks[:, 0:1] > 0
+    top = jnp.max(jnp.where(live, score, -1e30), axis=0, keepdims=True)
+    weight = jnp.where(live, jnp.exp(score - top), 0.0)
+    vector = jnp.sum(weight * embed, axis=0, keepdims=True)
+    payload = jnp.concatenate(
+        [vector[:, k * 128 : (k + 1) * 128] for k in range(lines)]
+        + [
+            jnp.broadcast_to(jnp.sum(weight, axis=0, keepdims=True), (1, 128)),
+            jnp.broadcast_to(top, (1, 128)),
+            jnp.zeros((SUB - lines - 2, 128), F32),
+        ],
+        axis=0,
+    )
 
     def combine(every):
         top = jnp.max(every[:, lines + 1 : lines + 2, :], axis=0)
@@ -292,13 +302,11 @@
         total = jnp.sum(every[:, : lines + 1, :] * factor, axis=0)
         return jnp.concatenate([total, top, jnp.zeros((SUB - lines - 2, 128), F32)], axis=0)
 
-    comb = exchanged(sizes, pay_ref[...], combine, rooms)
+    wait_greetings(sizes, True)
+    comb = exchanged(sizes, payload, combine, rooms)
     total, top = comb[lines : lines + 1, 0:1], comb[lines + 1 : lines + 2, 0:1]
     pooled = jnp.concatenate([comb[k : k + 1] for k in range(lines)], axis=1) / total
-    embed, tval, gval = embed_ref[...], tval_ref[...], gval_ref[...]
-    ao, cls = ao_ref[...], cls_ref[...]
-    live = live_ref[:, 0:1] > 0
-    prob = jnp.where(live, jnp.exp(score_ref[:, 0:1] - top), 0.0) / total
+    prob = jnp.where(live, jnp.exp(score - top), 0.0) / total
     gap = jnp.sum(embed * cls, axis=1, keepdims=True) - jnp.sum(pooled * cls, axis=1, keepdims=True)
     datt = (prob * gap) * ao
     dtanh = datt * gval * (1.0 - tval * tval)
@@ -310,17 +318,17 @@
         + lax.dot_general(dsigm, as_ref[...], back, precision=HP, preferred_element_type=F32)
     ) * (1.0 / (half * half))
     dembed_ref[...] = dembed
-    ocol, mid = row2_ref.shape
-    orow = col2_ref.shape[0]
+    ocol, mid = row2.shape
+    orow = col2.shape[0]
     we = wb_ref[:, :mid]
 
     def spread_rows(rows):
         return jnp.concatenate([jnp.broadcast_to(dembed[t : t + 1], (half, cout)) for t in rows], axis=0)
 
-    dpre = (row3_ref[...].astype(F32) * spread_rows(range(tiles_c))).astype(BF16)
-    edges[0:ocol, :] = (dot(dpre, we) * row2_ref[...].astype(F32)).astype(BF16)
-    dpre = (col3_ref[...] * spread_rows(range(0, tiles_r * tiles_c, tiles_c))).astype(BF16)
-    edges[ocol : ocol + orow, :] = (dot(dpre, we) * col2_ref[...]).astype(BF16)
+    dpre = (row3[...].astype(F32) * spread_rows(range(tiles_c))).astype(BF16)
+    edges[0:ocol, :] = (dot(dpre, we) * row2[...].astype(F32)).astype(BF16)
+    dpre = (col3[...] * spread_rows(range(0, tiles_r * tiles_c, tiles_c))).astype(BF16)
+    edges[ocol : ocol + orow, :] = (dot(dpre, we) * col2[...]).astype(BF16)
     spans = ((0, ocol, 0), (ocol, orow, ocol), (0, 2 * SUB, ocol + orow))
     targets = (peer(sizes, 1, sizes[1] - 1), peer(sizes, 0, sizes[0] - 1), corner_of(sizes, -1))
     copies = [
@@ -429,7 +437,6 @@
     orow, ocol = rows // 2, cols // 2
     delta = stain_delta[None, :]
     wc = spatial_weight.reshape(3, 3 * mid, mid)
-    live = jnp.pad((tissue.reshape(-1, 1) > 0).astype(F32), ((0, slots - tiles_r * tiles_c), (0, 127)))
     ao = attn_out[None, :]
     cls = classifier[None, :]
     sizes = tuple(lax.axis_size(axis) for axis in AXES)
@@ -476,22 +483,16 @@
 
     steps = rows // BLOCK
     params = pltpu.CompilerParams(dimension_semantics=("arbitrary",), vmem_limit_bytes=56 * 1024 * 1024)
-    slope1, slope2, slope3, row2, row3, col2, col3, pay, embed, tval, gval, score = pl.pallas_call(
-        functools.partial(forward_kernel, tiles_r, tiles_c),
+    slope1, slope2, slope3, dembed, low, right = pl.pallas_call(
+        functools.partial(forward_kernel, sizes),
         grid=(steps,),
         out_shape=(
             jax.ShapeDtypeStruct((rows, cols, mid), BF16),
             jax.ShapeDtypeStruct((orow, ocol, mid), BF16),
             jax.ShapeDtypeStruct((orow, ocol, cout), BF16),
-            jax.ShapeDtypeStruct((ocol, mid), BF16),
-            jax.ShapeDtypeStruct((ocol, cout), BF16),
+            jax.ShapeDtypeStruct((slots, cout), F32),
+            jax.ShapeDtypeStruct((ocol + SUB, mid), F32),
             jax.ShapeDtypeStruct((orow, mid), F32),
-            jax.ShapeDtypeStruct((orow, cout), F32),
-            jax.ShapeDtypeStruct((SUB, 128), F32),
-            jax.ShapeDtypeStruct((slots, cout), F32),
-            jax.ShapeDtypeStruct((slots, att), F32),
-            jax.ShapeDtypeStruct((slots, att), F32),
-            jax.ShapeDtypeStruct((slots, 128), F32),
         ),
         in_specs=[
             pl.BlockSpec((BLOCK, cols, chan), lambda i: (i, 0, 0)),
@@ -503,21 +504,17 @@
             whole(attn_tanh.shape),
             whole(attn_sigm.shape),
             whole(ao.shape),
-            whole(live.shape),
+            whole(cls.shape),
+            whole(wb.shape),
+            whole(tissue.shape),
         ],
         out_specs=(
             pl.BlockSpec((BLOCK, cols, mid), lambda i: (i, 0, 0)),
             pl.BlockSpec((BLOCK // 2, ocol, mid), lambda i: (i, 0, 0)),
             pl.BlockSpec((BLOCK // 2, ocol, cout), lambda i: (i, 0, 0)),
-            whole((ocol, mid)),
-            whole((ocol, cout)),
-            pl.BlockSpec((BLOCK // 2, mid), lambda i: (i, 0)),
-            pl.BlockSpec((BLOCK // 2, cout), lambda i: (i, 0)),
-            whole((SUB, 128)),
             whole((slots, cout)),
-            whole((slots, att)),
-            whole((slots, att)),
-            whole((slots, 128)),
+            whole((ocol + SUB, mid)),
+            whole((orow, mid)),
         ),
         scratch_shapes=[
             pltpu.VMEM((BLOCK, cols + SUB, mid), F32),
@@ -525,28 +522,24 @@
             pltpu.VMEM((BLOCK // 2, cols, chan // 2), F32),
             pltpu.VMEM((BLOCK + 1, ocol, 3 * mid), BF16),
             pltpu.VMEM((slots, SUB, cout), F32),
-        ],
-        compiler_params=params,
-        name="forward",
-    )(features, up, left, wr, wc, wp, attn_tanh, attn_sigm, ao, live)
-
-    dembed, low, right = pl.pallas_call(
-        functools.partial(edge_kernel, sizes, tiles_r, tiles_c),
-        out_shape=(
-            jax.ShapeDtypeStruct((slots, cout), F32),
-            jax.ShapeDtypeStruct((ocol + SUB, mid), F32),
-            jax.ShapeDtypeStruct((orow, mid), F32),
-        ),
-        scratch_shapes=[
+            pltpu.VMEM((ocol, mid), BF16),
+            pltpu.VMEM((ocol, cout), BF16),
+            pltpu.VMEM((orow, mid), F32),
+            pltpu.VMEM((orow, cout), F32),
             pltpu.VMEM((ocol + orow, mid), BF16),
             pltpu.VMEM((ocol + orow + 2 * SUB, mid), BF16),
             pltpu.SemaphoreType.DMA((3,)),
             pltpu.SemaphoreType.DMA((3,)),
         ]
         + exchange_rooms(sizes),
-        compiler_params=pltpu.CompilerParams(collective_id=0, has_side_effects=True),
-        name="edge",
-    )(pay, embed, tval, gval, score, live, ao, cls, attn_tanh, attn_sigm, wb, row3, row2, col3, col2)
+        compiler_params=pltpu.CompilerParams(
+            dimension_semantics=("arbitrary",),
+            vmem_limit_bytes=56 * 1024 * 1024,
+            collective_id=0,
+            has_side_effects=True,
+        ),
+        name="forward",
+    )(features, up, left, wr, wc, wp, attn_tanh, attn_sigm, ao, cls, wb, tissue)
 
     def turn(i):
         return (steps - 1 - i, 0, 0)

time: 72.8 us -> 67.1 us (0.922)
  Pallas kernels: 69.3 us -> 65 us
  other arithmetic: 2.48 us -> 1.2 us
    pallas_call x2 -> x1, Pallas kernels: 33.3 us -> 29.2 us  [shards(): pl.pallas_call(functools.partial(forward_kernel, sizes), grid=(steps,), o...]
where the time goes in v3:
time: 67.1 us; the launch traced here: 66.9 us
  Pallas kernels  65 us (97%)
  other arithmetic  1.2 us (2%)
    pallas_call x1, Pallas kernels, shards(): pl.pallas_call(functools.partial(forward_kernel, sizes), grid=(steps,), o...  29.2 us
    pallas_call x1, Pallas kernels, shards(): pl.pallas_call(functools.partial(backward_kernel, tiles_c), grid=(steps,)...  13.9 us
    pallas_call x1, Pallas kernels, shards(): pl.pallas_call(functools.partial(rim_kernel, sizes), grid=(1,), out_shape...  11.7 us
    pallas_call x1, Pallas kernels, shards(): pl.pallas_call(functools.partial(step_kernel, sizes), out_shape=jax.Shape...  10.3 us

profile of v3, /device:TPU:0, one launch (start us, length us, event | category | flops | bytes accessed | tf_op | source)
XLA Modules:
  0.0 66.9 jit_solution(2275714545490089760)
XLA Ops:
  0.6 11.7 %rim.1 = (f32[136,128]{1,0:T(8,128)}, f32[128,128]{1,0:T(8,128)}, bf16[256,128]{1,0:T(8,128)(2,1)}, bf16[384,512]{1,0:T(8,128)(2,1)}, bf16[512,384]{1,0:T(8,128)...) custom-call(bf16[128,128,256]{2,1,0:T(8,128)(2,1)} %x_ref.3, bf16[128,128,256]{2,1,0:T(8,128)(2,1)} %x_ref.3, ...), custom_call_target="tpu_custom_call" | custom-call | tf_op jit(solution)/shard_map/rim/pallas_call | solution.py:444
  12.3 29.2 %forward.1 = (bf16[128,128,128]{2,1,0:T(8,128)(2,1)}, bf16[64,64,128]{2,1,0:T(8,128)(2,1)}, bf16[64,64,512]{2,1,0:T(8,128)(2,1)}, f32[8,512]{1,0:T(8,128)}, f32[72,128]{1,0:T(8,128)}, /*index=5*/f32[64,128]{1,0:T(8,128)}) custom-call(bf16[128,128,256]{2,1,0:T(8,128)(2,1)} %x_ref.3, f32[136,128]{1,0:T(8,128)} %get-tuple-element.17.up_ref, ...), custom_call_target="tpu_custom_call" | custom-call | tf_op jit(solution)/shard_map/forward/pallas_call | solution.py:486
  41.5 0.0 copy-start
  41.5 13.9 %backward.1 = (bf16[128,128,256]{2,1,0:T(8,128)(2,1)}, f32[8,256]{1,0:T(8,128)}) custom-call(bf16[128,128,256]{2,1,0:T(8,128)(2,1)} %x_ref.3, bf16[128,128,128]{2,1,0:T(8,128)(2,1)} %get-tuple-element.22.slope1_ref, bf16[64,64,128]{2,1,0:T(8,128)(2,1)} %get-tuple-element.23.slope2_ref, bf16[64,64,512]{2,1,0:T(8,128)(2,1)} %get-tuple-element.24.slope3_ref, ...), custom_call_target="tpu_custom_call" | custom-call | tf_op jit(solution)/shard_map/backward/pallas_call | solution.py:547
  55.4 10.3 %step.1 = f32[1,256]{1,0:T(1,128)} custom-call(f32[8,256]{1,0:T(8,128)} %get-tuple-element.31.grad_ref, f32[1,256]{1,0:T(1,128)} %bitcast.8, s32[1,256]{1,0:T(1,128)} %bitcast.12), custom_call_target="tpu_custom_call" | custom-call | tf_op jit(solution)/shard_map/step/pallas_call | solution.py:577
  65.7 0.0 copy-done
  65.7 1.2 %add.3 = f32[256]{0:T(256)} add(f32[256]{0:T(256)S(1)} %copy-done, f32[256]{0:T(256)} %bitcast.9) | non-fusion elementwise | flops 256 | bytes 3072 | tf_op jit(solution)/shard_map/add | solution.py:577
Async XLA Ops:
  41.5 24.2 %copy-start = (f32[256]{0:T(256)S(1)}, f32[256]{0:T(256)}, u32[]{:S(2)}) copy-start(f32[256]{0:T(256)} %param.13) | copy-start | bytes 3076
